TPU v7x, 256 devices: a whole 4x4x8 slice. The times are simulated.
256 devices in a mesh: dp: 16 (over x, z_lo), shard: 16 (over z_hi, y, core).
Axes of the slice: x: 4, y: 4, z: 8 (z_hi: 2, z_lo: 4; z = z_hi * 4 + z_lo), core: 2. Of those that a mesh axis runs over, the one named last changes fastest.
Arguments:
- codes: int32 [16, 5, 8, 64], P('dp', None, None, 'shard'), may hold values from 0 to 262143
- lengths: int32 [16], P('dp'), may hold values from 1 to 5, 48 in all
- hidden: bfloat16 [16, 5, 8, 64, 512], P('dp', None, None, 'shard'), may hold values from -6 to 6
- embed: bfloat16 [18, 512], replicated, may hold values from -1.5 to 1.5
- conv_weight: bfloat16 [512, 27, 512], P('shard'), may hold values from -0.0546875 to 0.0546875
- gain: float32 [512], replicated, may hold values from 0.1 to 1.9
- bias: float32 [512], replicated, may hold values from -3 to 3
- cotangent: bfloat16 [16, 5, 16, 128, 128], P('dp', None, None, 'shard'), may hold values from -6 to 6
Outputs:
- decoded: bfloat16 [16, 5, 16, 128, 128], P('dp', None, None, 'shard')
- grad_hidden: bfloat16 [16, 5, 8, 64, 512], P('dp', None, None, 'shard')
- grad_conv: float32 [512, 27, 512], P('shard')
- grad_embed: float32 [18, 512], replicated
- grad_gain: float32 [512], replicated
- grad_bias: float32 [512], replicated
Inputs may be any that keep to these rules, and one draw needn't show every extreme that they name: Frames from lengths[c] on are padding; some clip has all 5 frames valid.
All inputs are finite; a program needn't handle non-finite values. No bound on the sum of `lengths` on one device may be relied on, other than what follows from the above.
Results may differ from a plain program's by a relative error of at most 0.02.
Values may be sent and summed in bfloat16 or wider, within the bound.
A program may use at most 128 MiB of HBM per device.

v0:
```python
import jax
import jax.numpy as jnp
from jax import lax
from jax.sharding import PartitionSpec as P

CODE_BITS = 18
GROUPS = 32


eps_norm = 1e-05


def forward_taps(padded, frames, height, width):
    taps = []
    for depth_tap in range(3):
        for row_tap in range(3):
            for col_tap in range(3):
                taps.append(
                    padded[
                        depth_tap : depth_tap + frames,
                        row_tap : row_tap + height,
                        col_tap : col_tap + width,
                    ]
                )
    return taps


def backward_taps(padded, frames, height, width):
    taps = []
    for depth_tap in range(3):
        for row_tap in range(3):
            for col_tap in range(3):
                taps.append(
                    padded[
                        2 - depth_tap : 2 - depth_tap + frames,
                        2 - row_tap : 2 - row_tap + height,
                        2 - col_tap : 2 - col_tap + width,
                    ]
                )
    return taps


def slab_columns(spread, frames, height, slab_width):
    padded = jnp.pad(spread, ((2, 0), (1, 1), (1, 1), (0, 0)))
    return jnp.concatenate(forward_taps(padded, frames, height, slab_width), axis=3)


def on_device(codes, lengths, hidden, embed, conv_weight, gain, bias, cotangent):
    frames = codes.shape[1]
    height = codes.shape[2]
    width = codes.shape[3]
    share = conv_weight.shape[0]
    channels = conv_weight.shape[2]
    quarter = channels // 4
    shards = lax.axis_size("shard")
    slab_width = width * shards
    positions = frames * height * width
    groups = GROUPS
    per_group = channels // groups
    frame_mask = (jnp.arange(frames) < lengths[0]).astype(jnp.float32)
    mask_cells = frame_mask[:, None, None, None]
    mask_groups = frame_mask[:, None, None, None, None]
    powers = 2 ** jnp.arange(CODE_BITS, dtype=jnp.int32)
    bits = (codes[0][..., None] // powers % 2 * 2 - 1).astype(jnp.bfloat16)
    embedded = jnp.dot(
        bits.reshape(positions, CODE_BITS), embed, preferred_element_type=jnp.float32
    ).reshape(frames, height, width, channels)
    features = ((embedded + hidden[0].astype(jnp.float32)) * mask_cells).astype(jnp.bfloat16)
    spread = lax.all_to_all(features, "shard", split_axis=3, concat_axis=2, tiled=True)
    slab_patches = slab_columns(spread, frames, height, slab_width)
    flat_share = jnp.transpose(conv_weight, (1, 0, 2)).reshape(27 * share, channels)
    part_sums = jnp.dot(
        slab_patches.reshape(-1, 27 * share), flat_share, preferred_element_type=jnp.float32
    ).reshape(frames, height, slab_width, channels)
    conv_out = lax.psum_scatter(
        part_sums.astype(jnp.bfloat16), "shard", scatter_dimension=2, tiled=True
    ).astype(jnp.float32)
    grouped = conv_out.reshape(frames, height, width, groups, per_group)
    sum_one, sum_two = lax.psum(
        (
            jnp.sum(grouped * mask_groups, axis=(0, 1, 2, 4)),
            jnp.sum(grouped * grouped * mask_groups, axis=(0, 1, 2, 4)),
        ),
        "shard",
    )
    count = lengths[0].astype(jnp.float32) * (height * width * shards * per_group)
    mean = sum_one / count
    variance = sum_two / count - mean * mean
    inv_std = lax.rsqrt(variance + eps_norm)
    gain_group = gain.reshape(groups, per_group)
    bias_group = bias.reshape(groups, per_group)
    normed = (grouped - mean[:, None]) * inv_std[:, None]
    pre = normed * gain_group + bias_group
    sigma = jax.nn.sigmoid(pre)
    activated = pre * sigma * mask_groups
    decoded = (
        activated.reshape(frames, height, width, 2, 2, quarter)
        .transpose(0, 1, 3, 2, 4, 5)
        .reshape(frames, 2 * height, 2 * width, quarter)
        .astype(jnp.bfloat16)[None]
    )
    upstream = (
        cotangent[0]
        .astype(jnp.float32)
        .reshape(frames, height, 2, width, 2, quarter)
        .transpose(0, 1, 3, 2, 4, 5)
        .reshape(frames, height, width, groups, per_group)
        * mask_groups
    )
    d_pre = upstream * sigma * (1.0 + pre * (1.0 - sigma))
    gain_term = jnp.sum(d_pre * normed, axis=(0, 1, 2)).reshape(channels)
    bias_term = jnp.sum(d_pre, axis=(0, 1, 2)).reshape(channels)
    d_norm = d_pre * gain_group
    tot_one, tot_two = lax.psum(
        (jnp.sum(d_norm, axis=(0, 1, 2, 4)), jnp.sum(d_norm * normed, axis=(0, 1, 2, 4))), "shard"
    )
    d_conv = (
        (
            inv_std[:, None]
            * (d_norm - tot_one[:, None] / count - normed * tot_two[:, None] / count)
            * mask_groups
        )
        .reshape(frames, height, width, channels)
        .astype(jnp.bfloat16)
    )
    whole_grad = lax.all_gather(d_conv, "shard", axis=2, tiled=True)
    back_share = jnp.transpose(conv_weight, (2, 1, 0)).reshape(channels, 27 * share)
    tap_images = jnp.dot(
        whole_grad.reshape(-1, channels), back_share, preferred_element_type=jnp.float32
    ).reshape(frames, height, slab_width, 27 * share)
    padded_images = jnp.pad(tap_images, ((0, 2), (1, 1), (1, 1), (0, 0)))
    input_sum = jnp.zeros((frames, height, slab_width, share), jnp.float32)
    for tap_index, shifted in enumerate(backward_taps(padded_images, frames, height, slab_width)):
        input_sum = input_sum + shifted[..., tap_index * share : (tap_index + 1) * share]
    d_features = lax.all_to_all(
        input_sum.astype(jnp.bfloat16), "shard", split_axis=2, concat_axis=3, tiled=True
    )
    clip_part = jnp.einsum(
        "pk,pc->kc",
        slab_patches.reshape(-1, 27 * share),
        whole_grad.reshape(-1, channels),
        preferred_element_type=jnp.float32,
    )
    weight_sum = clip_part.reshape(27, share, channels).transpose(1, 0, 2)
    grad_conv = lax.psum(weight_sum.astype(jnp.bfloat16), "dp").astype(jnp.float32)
    grad_hidden = d_features * mask_cells.astype(jnp.bfloat16)
    embed_term = jnp.dot(
        bits.reshape(positions, CODE_BITS).T,
        grad_hidden.reshape(positions, channels),
        preferred_element_type=jnp.float32,
    )
    grad_embed, grad_gain, grad_bias = lax.psum((embed_term, gain_term, bias_term), ("dp", "shard"))
    return (decoded, grad_hidden[None], grad_conv, grad_embed, grad_gain, grad_bias)


def solution(mesh):
    return jax.shard_map(
        on_device,
        mesh=mesh,
        in_specs=(
            P("dp", None, None, "shard"),
            P("dp"),
            P("dp", None, None, "shard", None),
            P(),
            P("shard", None, None),
            P(),
            P(),
            P("dp", None, None, "shard", None),
        ),
        out_specs=(
            P("dp", None, None, "shard", None),
            P("dp", None, None, "shard", None),
            P("shard", None, None),
            P(),
            P(),
            P(),
        ),
        check_vma=False,
    )
```

profile of v0, /device:TPU:8, one launch (start us, length us, event | category | flops | bytes accessed | tf_op | source)
XLA Modules:
  0.0 610.6 jit_solution(5969993515602103230)
XLA Ops:
  8.7 2.7 fusion.29
  11.4 2.6 copy.34
  14.0 3.4 reshape.359
  17.4 20.4 %all_to_all.39 = bf16[16,2,2560]{2,1,0:T(2,128)(2,1)S(1)} all-to-all(bf16[16,2,2560]{2,1,0:T(2,128)(2,1)} %reshape.359), channel_id=1, replica_groups=mesh['dp'=16,'shard'=16] {'shard'}, dimensions={0} | all-to-all | bytes 327680 | tf_op jit(solution)/shard_map/all_to_all | solution.py:69
  37.8 4.1 reshape.360
  41.9 4.3 copy.35
  46.3 2.9 pad_slice_fusion.27
  49.2 6.8 %pad_slice_fusion.26 = (bf16[5,8,64,32]{3,2,1,0:T(8,128)(2,1)S(1)}, bf16[5,8,64,32]{3,2,1,0:T(8,128)(2,1)S(1)}, bf16[5,8,64,32]{3,2,1,0:T(8,128)(2,1)S(1)}, bf16...) fusion(bf16[5,8,64,32]{3,2,1,0:T(8,128)(2,1)S(1)} %bitcast.128), kind=kLoop, calls=%fused_computation.26 | loop fusion | bytes 3276800 | tf_op jit(solution)/shard_map/slice | solution.py:19
  56.0 16.7 %concatenate.61 = bf16[5,8,64,864]{3,2,1,0:T(8,128)(2,1)} concatenate(bf16[5,8,64,32]{3,2,1,0:T(8,128)(2,1)} %get-tuple-element.46, bf16[5,8,64,32]{3,2,1,0:T(8,128)(2,1)S(1)} %get-tuple-element.22, bf16[5,8,64,32]{3,2,1,0:T(8,128)(2,1)S(1)} %get-tuple-element.23, bf16[5,8,64,32]{3,2,1,0:T(8,128)(2,1)} %get-tuple-element.24, bf16[5,8,64,32]{3,2,1,0:T(8,128)(2,1)} %get-tuple-element.25, ...), dimensions={3} | concatenate | bytes 8847360 | tf_op jit(solution)/shard_map/concatenate | solution.py:45
  72.7 5.4 convolution_convert_fusion
  78.1 3.0 copy.36
  81.2 1.7 copy.38
  82.9 1.8 convert.7
  85.9 172.9 %all-reduce.11.cloned.1.call-done = bf16[5,8,64,512]{3,1,2,0:T(8,128)(2,1)} async-done(((bf16[5,8,64,512]{3,1,2,0:T(8,128)(2,1)}), bf16[5,8,64,512]{3,1,2,0:T(8,128)(2,1)}) %all-reduce.11.cloned.1.call-update) | async-done | bytes 2621456
  258.9 1.6 multiply_reduce_fusion.2
  262.1 50.1 %all-reduce.5 = (f32[32]{0:T(128)S(1)}, f32[32]{0:T(128)S(1)}) all-reduce(f32[32]{0:T(128)S(1)} %reduce_sum.67, f32[32]{0:T(128)} %reduce_sum.73), channel_id=1, replica_groups=mesh['dp'=16,'shard'=16] {'shard'}, use_global_device_ids=true, to_apply=%region_3.4 | all-reduce | flops 64 | bytes 512 | tf_op jit(solution)/shard_map/psum | solution.py:79
  315.5 1.9 fusion.31
  320.4 42.9 %all-reduce.4 = (f32[32]{0:T(128)S(1)}, f32[32]{0:T(128)S(1)}) all-reduce(f32[32]{0:T(128)S(1)} %reduce_sum.93, f32[32]{0:T(128)} %reduce_sum.90), channel_id=1, replica_groups=mesh['dp'=16,'shard'=16] {'shard'}, use_global_device_ids=true, to_apply=%region_12.13 | all-reduce | flops 64 | bytes 512 | tf_op jit(solution)/shard_map/psum | solution.py:114
  363.6 2.0 multiply_convert_fusion
  365.6 16.7 %concatenate.89 = bf16[2560,864]{1,0:T(8,128)(2,1)} concatenate(bf16[2560,32]{1,0:T(8,128)(2,1)} %bitcast.158, bf16[2560,32]{1,0:T(8,128)(2,1)S(1)} %bitcast.134, bf16[2560,32]{1,0:T(8,128)(2,1)S(1)} %bitcast.135, bf16[2560,32]{1,0:T(8,128)(2,1)} %bitcast.136, bf16[2560,32]{1,0:T(8,128)(2,1)} %bitcast.137, bf16[2560,32]{1,0:T(8,128)(2,1)} %bitcast.138, ...), dimensions={1} | concatenate | bytes 8847360 | tf_op jit(solution)/shard_map/concatenate | solution.py:45
  382.4 7.3 %copy.42 = bf16[864,2560]{1,0:T(8,128)(2,1)} copy(bf16[864,2560]{0,1:T(8,128)(2,1)} %bitcast.126) | data formatting | bytes 8847360 | tf_op jit(solution)/shard_map/pk,pc->kc/dot_general | solution.py:138
  389.6 43.9 %all-gather.2.cloned.1.call-done = bf16[5,8,64,512]{3,1,2,0:T(8,128)(2,1)} async-done(((bf16[5,8,4,512]{3,1,2,0:T(8,128)(2,1)}), bf16[5,8,64,512]{3,1,2,0:T(8,128)(2,1)}) %all-gather.2.cloned.1.call-update) | async-done | bytes 2621456 | tf_op jit(solution)/shard_map/all_gather | solution.py:126
  433.6 2.8 copy.39
  436.6 3.4 fusion
  440.0 3.1 fusion.55
  443.1 6.2 %fusion.27 = bf16[5,8,64,32]{3,2,1,0:T(8,128)(2,1)S(1)} fusion(f32[5,8,64,864]{3,2,1,0:T(8,128)S(1)} %fusion.55), kind=kLoop, calls=%fused_computation.81 | loop fusion | flops 2211840 | bytes 10649600 | tf_op jit(solution)/shard_map/convert_element_type | solution.py:136
  449.8 1.2 reshape.361
  450.9 4.5 all-to-all-start.1
  456.2 8.4 %all-to-all-done.1 = bf16[16,2,2560]{2,1,0:T(2,128)(2,1)S(1)} async-done(((bf16[16,2,2560]{2,1,0:T(2,128)(2,1)}), bf16[16,2,2560]{2,1,0:T(2,128)(2,1)S(1)}, u32[]{:S(2)}, u32[]{:S(2)}) %all-to-all-start.1) | async-done | bytes 163872 | tf_op jit(solution)/shard_map/all_to_all | solution.py:135
  467.8 79.0 %all-reduce.3 = (f32[18,512]{1,0:T(8,128)}, f32[512]{0:T(512)}, f32[512]{0:T(512)}) all-reduce(f32[18,512]{1,0:T(8,128)S(1)} %convolution_bitcast_fusion, f32[512]{0:T(512)S(1)} %bitcast.175, f32[512]{0:T(512)S(1)} %bitcast.176), channel_id=1, replica_groups=mesh['dp'=16,'shard'=16] {'dp','shard'}, use_global_device_ids=true, to_apply=%region_14.15 | all-reduce | flops 10240 | bytes 81920 | tf_op jit(solution)/shard_map/psum | solution.py:152
  547.6 53.8 %all-reduce.9.cloned.1.call-done = bf16[32,27,512]{2,0,1:T(8,128)(2,1)} async-done(((bf16[32,27,512]{2,0,1:T(8,128)(2,1)}), bf16[32,27,512]{2,0,1:T(8,128)(2,1)}) %all-reduce.9.cloned.1.call-update) | async-done | bytes 884752 | tf_op jit(solution)/shard_map/psum | solution.py:145
  601.4 2.6 convert_element_type.102
  (78 shorter events, 15.0 us)
Async XLA Ops:
  7.2 65.5 %copy-start = (bf16[32,27,512]{2,0,1:T(8,128)(2,1)S(1)}, bf16[32,27,512]{2,0,1:T(8,128)(2,1)}, u32[]{:S(2)}) copy-start(bf16[32,27,512]{2,0,1:T(8,128)(2,1)} %param.12) | copy-start | bytes 2654212
  7.2 251.7 %all-reduce.11.cloned.1.call-start = ((), (), s32[]{:S(2)}) async-start(), calls=%async_computation.4 | async-start | bytes 5242880
  7.2 6.7 %copy-start.12 = (s32[18]{0:T(128)}, s32[18]{0:T(128)S(1)}, u32[]{:S(2)}) copy-start(s32[18]{0:T(128)S(1)} %get-tuple-element.49) | copy-start | bytes 220
  7.3 6.7 %copy-start.14 = (s32[18]{0:T(128)}, s32[18]{0:T(128)S(1)}, u32[]{:S(2)}) copy-start(s32[18]{0:T(128)S(1)} %get-tuple-element.50) | copy-start | bytes 220
  8.0 250.9 %copy-start.9 = (f32[5]{0:T(128)}, f32[5]{0:T(128)S(1)}, u32[]{:S(2)}) copy-start(f32[5]{0:T(128)S(1)} %compare_convert_fusion) | copy-start | bytes 64
  81.1 3.6 copy-start.11
  81.1 234.4 %copy-start.4 = (f32[512]{0:T(512)S(1)}, f32[512]{0:T(512)}, u32[]{:S(2)}) copy-start(f32[512]{0:T(512)} %param.13) | copy-start | bytes 6148
  81.2 352.4 %all-gather.2.cloned.1.call-start = ((), (), s32[]{:S(2)}) async-start(), calls=%async_computation.2 | async-start | bytes 2785280 | tf_op jit(solution)/shard_map/all_gather | solution.py:126
  312.1 0.5 copy-start.10
  312.7 50.9 %copy-start.6 = (f32[512]{0:T(512)S(1)}, f32[512]{0:T(512)}, u32[]{:S(2)}) copy-start(f32[512]{0:T(512)} %param.14) | copy-start | bytes 6148
  365.6 235.9 %all-reduce.9.cloned.1.call-start = ((), (), s32[]{:S(2)}) async-start(), calls=%async_computation.3 | async-start | bytes 1769472 | tf_op jit(solution)/shard_map/psum | solution.py:145
  433.6 3.0 copy-start.1
  436.6 3.4 copy-start.2
  449.3 6.1 %copy-start.3 = (bf16[5,8,2,4,2,128]{5,1,4,2,3,0:T(8,128)(2,1)S(1)}, bf16[5,8,2,4,2,128]{5,1,4,2,3,0:T(8,128)(2,1)}, u32[]{:S(2)}) copy-start(bf16[5,8,2,4,2,128]{5,1,4,2,3,0:T(8,128)(2,1)} %get-tuple-element.48) | copy-start | bytes 491524
  450.9 13.8 %all-to-all-start.1 = ((bf16[16,2,2560]{2,1,0:T(2,128)(2,1)}), bf16[16,2,2560]{2,1,0:T(2,128)(2,1)S(1)}, u32[]{:S(2)}, u32[]{:S(2)}) async-start(bf16[16,2,2560]{2,1,0:T(2,128)(2,1)} %reshape.361), calls=%async_computation.1 | async-start | bytes 327680 | tf_op jit(solution)/shard_map/all_to_all | solution.py:135
  465.3 1.4 copy-start.5
  465.3 1.4 copy-start.13
  465.3 1.4 copy-start.15
  465.6 2.2 copy-start.7
  465.6 2.2 copy-start.8
Sparse Core Ops, SparseCore 0:
  81.3 177.5 all-reduce.10
  365.7 67.8 all-gather.1
  440.1 161.2 all-reduce.8
where the time goes:
time: 615 us; the launch traced here: 611 us
  waiting for transfers between devices  279 us (45%)
  blocking collectives  192 us (31%)
  local copies, waits for them, and re-layouts  82.7 us (13%)
  other arithmetic  20.8 us (3%)
  matrix products  15.5 us (3%)
  between operations  15.4 us (3%)
    unnamed x4, waiting for transfers between devices  173 us
    psum x1, blocking collectives, on_device(): lax.psum((embed_term, gain_term, bias_term), ('dp', 'shard'))  79 us
    psum x1, waiting for transfers between devices, on_device(): lax.psum(weight_sum.astype(jnp.bfloat16), 'dp').astype(jnp.float32)  53.8 us
    psum x1, blocking collectives, on_device(): lax.psum((jnp.sum(grouped * mask_groups, axis=(0, 1, 2, 4)), jnp.sum(grou...  50.1 us
    all_gather x1, waiting for transfers between devices, on_device(): whole_grad = lax.all_gather(d_conv, 'shard', axis=2, tiled=True)  43.9 us
    psum x1, blocking collectives, on_device(): lax.psum((jnp.sum(d_norm, axis=(0, 1, 2, 4)), jnp.sum(d_norm * normed, ax...  42.9 us
    concatenate x2, local copies, waits for them, and re-layouts, slab_columns(): jnp.concatenate(forward_taps(padded, frames, height, slab_width), axis=3)  33.4 us
    all_to_all x1, blocking collectives, on_device(): lax.all_to_all(features, 'shard', split_axis=3, concat_axis=2, tiled=True)  20.4 us
  transfers between devices with their start and end apart: 4, of which 4 were waited for; matrix products, arithmetic and copies ran while one was open for 7% of the time, Pallas kernels for 0%

commit v1 on v0

v1 whole, which is shorter than its diff:
```python
import jax
import jax.numpy as jnp
from jax import lax
from jax.experimental import pallas as pl
from jax.experimental.pallas import tpu as pltpu
from jax.sharding import PartitionSpec as P

BF = jnp.bfloat16
F32 = jnp.float32
CODE_BITS = 18
EPS = 1e-05
T = 5
R = 8
WD = 4
NS = 16
LP = 512
G = 7
MESH = pl.DeviceIdType.MESH
VM = pl.BlockSpec(memory_space=pltpu.VMEM)


def params(cid=None):
    if cid is None:
        return pltpu.CompilerParams(vmem_limit_bytes=60 * 1024 * 1024)
    return pltpu.CompilerParams(
        vmem_limit_bytes=60 * 1024 * 1024, collective_id=cid, has_side_effects=True
    )


def shard_spot():
    me = lax.axis_index("shard")
    return me, me // 8, (me // 2) % 4, me % 2


def sid(z, y, c):
    return z * 8 + y * 2 + c


def barrier(targets):
    sem = pltpu.get_barrier_semaphore()
    for axis, peer in targets:
        pl.semaphore_signal(sem, inc=1, device_id={axis: peer}, device_id_type=MESH)
    pl.semaphore_wait(sem, len(targets))


def rcopy(src, dst, ssem, rsem, axis, peer):
    return pltpu.make_async_remote_copy(
        src_ref=src, dst_ref=dst, send_sem=ssem, recv_sem=rsem,
        device_id={axis: peer}, device_id_type=MESH,
    )


def a2a_body(src, dst, ssem, rsem):
    me = lax.axis_index("shard")
    barrier([("shard", (me + d) % NS) for d in range(1, NS)])
    sends = []
    for d in range(1, NS):
        peer = (me + d) % NS
        cp = rcopy(src.at[peer], dst.at[me], ssem.at[d], rsem.at[d], "shard", peer)
        cp.start()
        sends.append(cp)
    dst[me] = src[me]
    for d in range(1, NS):
        frm = (me + NS - d) % NS
        rcopy(src.at[frm], dst.at[frm], ssem.at[d], rsem.at[d], "shard", frm).wait_recv()
    for cp in sends:
        cp.wait_send()


def exchange_in(blocks):
    return pl.pallas_call(
        a2a_body,
        out_shape=jax.ShapeDtypeStruct(blocks.shape, blocks.dtype),
        in_specs=[VM], out_specs=VM,
        scratch_shapes=[pltpu.SemaphoreType.DMA((NS,)), pltpu.SemaphoreType.DMA((NS,))],
        compiler_params=params(0),
        name="exchange_in",
    )(blocks)


def lane_masks():
    lane = lax.broadcasted_iota(jnp.int32, (1, LP), 1)
    row = (lane // 4) % 8
    col = lane % 4
    return {
        "r0": row >= 1, "r2": row <= 6,
        "c0": col >= 1, "c2": col <= 2,
        "w0": lane % 4 + lane // 32 > 0, "w2": lane % 4 + 4 * (lane // 32) < 63,
    }


def row_shift(x, d, m):
    if d < 0:
        return jnp.where(m["r0"], pltpu.roll(x, 4, 1), 0.0)
    if d > 0:
        return jnp.where(m["r2"], pltpu.roll(x, LP - 4, 1), 0.0)
    return x


def col_shift(x, d, m):
    if d < 0:
        y = jnp.where(m["c0"], pltpu.roll(x, 1, 1), pltpu.roll(x, 29, 1))
        return jnp.where(m["w0"], y, 0.0)
    if d > 0:
        y = jnp.where(m["c2"], pltpu.roll(x, LP - 1, 1), pltpu.roll(x, LP - 29, 1))
        return jnp.where(m["w2"], y, 0.0)
    return x


def dot(a, b):
    return lax.dot_general(a, b, (((1,), (0,)), ((), ())), preferred_element_type=F32)


def dot_nt(a, b):
    return lax.dot_general(a, b, (((1,), (1,)), ((), ())), preferred_element_type=F32)


def forward_body(g_ref, wt_ref, part_ref, ut_ref, bt_ref, pat_ref):
    m = lane_masks()
    eye = (
        lax.broadcasted_iota(jnp.int32, (128, 128), 0)
        == lax.broadcasted_iota(jnp.int32, (128, 128), 1)
    ).astype(F32).astype(BF)
    for t in range(T):
        rows = g_ref[:, t * 32:(t + 1) * 32, :].reshape(LP, 128)
        tt = dot_nt(eye, rows)
        ut_ref[t] = tt[64:96].astype(BF)
        bt_ref[t] = tt[96:128].astype(BF)
        f = tt[0:64]
        for dw in range(3):
            fc = col_shift(f, dw - 1, m)
            for dr in range(3):
                k = 3 * dr + dw
                pat_ref[t, 64 * k:64 * (k + 1), :] = row_shift(fc, dr - 1, m).astype(BF)
    for t in range(T):
        acc = None
        for dt in range(3):
            if t - 2 + dt < 0:
                continue
            d = dot(wt_ref[dt], pat_ref[t - 2 + dt])
            acc = d if acc is None else acc + d
        for k in range(8):
            part_ref[k, t] = acc[32 * k:32 * (k + 1)].astype(BF)


def forward(g, wt):
    return pl.pallas_call(
        forward_body,
        out_shape=(
            jax.ShapeDtypeStruct((8, T, 32, LP), BF),
            jax.ShapeDtypeStruct((T, 32, LP), BF),
            jax.ShapeDtypeStruct((T, 32, LP), BF),
            jax.ShapeDtypeStruct((T, 576, LP), BF),
        ),
        in_specs=[VM, VM], out_specs=(VM,) * 4,
        compiler_params=params(), name="forward",
    )(g, wt)


def scatter_body(p_ref, out_ref, rx1, tx2, rx2, txz, rxz, ssem, rsem):
    me, z, y, c = shard_spot()
    yp, ym = (y + 1) % 4, (y + 3) % 4
    up, down, over = sid(z, yp, c), sid(z, ym, c), sid(1 - z, y, c)
    barrier([("shard", up), ("shard", down), ("shard", over)])
    far = (y + 2) % 4

    def c1(t):
        return (
            rcopy(p_ref.at[:, far, t, pl.ds(0, 16)], rx1.at[0, t], ssem.at[0, t], rsem.at[0, t], "shard", up),
            rcopy(p_ref.at[:, far, t, pl.ds(16, 16)], rx1.at[1, t], ssem.at[1, t], rsem.at[1, t], "shard", down),
        )

    def c2(t):
        return (
            rcopy(tx2.at[0, t], rx2.at[0, t], ssem.at[2, t], rsem.at[2, t], "shard", up),
            rcopy(tx2.at[1, t], rx2.at[1, t], ssem.at[3, t], rsem.at[3, t], "shard", down),
        )

    def c3(t):
        return rcopy(txz.at[t], rxz.at[t], ssem.at[4, t], rsem.at[4, t], "shard", over)

    def s1(t):
        for cp in c1(t):
            cp.start()

    def s2(t):
        a, b = c1(t)
        n, q = c2(t)
        a.wait_recv()
        tx2[0, t, :, 0:16] = (p_ref[:, yp, t, 0:16].astype(F32) + rx1[0, t].astype(F32)).astype(BF)
        tx2[0, t, :, 16:32] = p_ref[:, yp, t, 16:32]
        n.start()
        b.wait_recv()
        tx2[1, t, :, 16:32] = (p_ref[:, ym, t, 16:32].astype(F32) + rx1[1, t].astype(F32)).astype(BF)
        tx2[1, t, :, 0:16] = p_ref[:, ym, t, 0:16]
        q.start()

    def s3(t):
        n, q = c2(t)
        n.wait_recv()
        q.wait_recv()
        txz[t] = (
            p_ref[1 - z, y, t].astype(F32) + rx2[0, t, 1 - z].astype(F32) + rx2[1, t, 1 - z].astype(F32)
        ).astype(BF)
        c3(t).start()
        out_ref[t] = p_ref[z, y, t].astype(F32) + rx2[0, t, z].astype(F32) + rx2[1, t, z].astype(F32)

    def s4(t):
        c3(t).wait_recv()
        out_ref[t] = out_ref[t] + rxz[t].astype(F32)

    stages = (s1, s2, s3, s4)
    for step in range(T + 3):
        for k in range(4):
            t = step - k
            if 0 <= t < T:
                stages[k](t)
    for t in range(T):
        for cp in c1(t) + c2(t) + (c3(t),):
            cp.wait_send()


def scatter(part):
    return pl.pallas_call(
        scatter_body,
        out_shape=jax.ShapeDtypeStruct((T, 32, LP), F32),
        in_specs=[VM], out_specs=VM,
        scratch_shapes=[
            pltpu.VMEM((2, T, 2, 16, LP), BF),
            pltpu.VMEM((2, T, 2, 32, LP), BF),
            pltpu.VMEM((2, T, 2, 32, LP), BF),
            pltpu.VMEM((T, 32, LP), BF),
            pltpu.VMEM((T, 32, LP), BF),
            pltpu.SemaphoreType.DMA((5, T)),
            pltpu.SemaphoreType.DMA((5, T)),
        ],
        compiler_params=params(1), name="scatter",
    )(part)


def group_sum(x):
    s = jnp.sum(x, axis=1, keepdims=True)
    g = jnp.sum(s.reshape(2, 16, 1), axis=1, keepdims=True)
    return jnp.broadcast_to(g, (2, 16, 1)).reshape(32, 1)


def norm_body(len_ref, conv_ref, ut_ref, gain_ref, bias_ref, act_ref, dc_ref, gb_ref, nrm, dpr):
    length = len_ref[0]
    count = length.astype(F32) * (R * WD * NS * 16)
    masks = [jnp.where(t < length, 1.0, 0.0) for t in range(T)]
    s1 = jnp.zeros((32, LP), F32)
    s2 = jnp.zeros((32, LP), F32)
    for t in range(T):
        v = conv_ref[t] * masks[t]
        s1 = s1 + v
        s2 = s2 + conv_ref[t] * v
    mean = group_sum(s1) / count
    var = group_sum(s2) / count - mean * mean
    inv = lax.rsqrt(var + EPS)
    gain = gain_ref[...]
    bias = bias_ref[...]
    a1 = jnp.zeros((32, LP), F32)
    a2 = jnp.zeros((32, LP), F32)
    for t in range(T):
        n = (conv_ref[t] - mean) * inv
        pre = n * gain + bias
        sg = jax.nn.sigmoid(pre)
        act_ref[t] = (pre * sg * masks[t]).astype(BF)
        dp = ut_ref[t].astype(F32) * masks[t] * sg * (1.0 + pre * (1.0 - sg))
        a1 = a1 + dp
        a2 = a2 + dp * n
        nrm[t] = n
        dpr[t] = dp
    bterm = jnp.sum(a1, axis=1, keepdims=True)
    gterm = jnp.sum(a2, axis=1, keepdims=True)
    t1 = group_sum(gain * bterm) / count
    t2 = group_sum(gain * gterm) / count
    for t in range(T):
        dc_ref[t] = (inv * (dpr[t] * gain - t1 - nrm[t] * t2) * masks[t]).astype(BF)
    lane = lax.broadcasted_iota(jnp.int32, (32, 128), 1)
    gb_ref[...] = jnp.where(lane == 0, gterm, jnp.where(lane == 1, bterm, 0.0))


def norm(lengths, conv, ut, gain, bias):
    return pl.pallas_call(
        norm_body,
        out_shape=(
            jax.ShapeDtypeStruct((T, 32, LP), BF),
            jax.ShapeDtypeStruct((T, 32, LP), BF),
            jax.ShapeDtypeStruct((32, 128), F32),
        ),
        in_specs=[pl.BlockSpec(memory_space=pltpu.SMEM), VM, VM, VM, VM],
        out_specs=(VM,) * 3,
        scratch_shapes=[pltpu.VMEM((T, 32, LP), F32), pltpu.VMEM((T, 32, LP), F32)],
        compiler_params=params(), name="norm",
    )(lengths, conv, ut, gain, bias)


def gather_body(own, out, ssem, rsem):
    me, z, y, c = shard_spot()
    o = 1 - z
    yp, ym = (y + 1) % 4, (y + 3) % 4
    up, down, over = sid(z, yp, c), sid(z, ym, c), sid(o, y, c)
    barrier([("shard", up), ("shard", down), ("shard", over)])
    lo, hi = pl.ds(0, 16), pl.ds(16, 16)

    def cp(kind, t, src, dst, peer):
        return rcopy(src, dst, ssem.at[kind, t], rsem.at[kind, t], "shard", peer)

    def send(kind, t):
        if kind == 0:
            return cp(0, t, own.at[t], out.at[z, y, t], over)
        if kind == 1:
            return cp(1, t, own.at[t], out.at[z, y, t], up)
        if kind == 2:
            return cp(2, t, own.at[t], out.at[z, y, t], down)
        if kind == 3:
            return cp(3, t, out.at[z, ym, t, lo], out.at[z, ym, t, lo], up)
        if kind == 4:
            return cp(4, t, out.at[z, yp, t, hi], out.at[z, yp, t, hi], down)
        if kind == 5:
            return cp(5, t, out.at[o, y, t], out.at[o, y, t], up)
        if kind == 6:
            return cp(6, t, out.at[o, y, t], out.at[o, y, t], down)
        if kind == 7:
            return cp(7, t, out.at[o, ym, t, lo], out.at[o, ym, t, lo], up)
        return cp(8, t, out.at[o, yp, t, hi], out.at[o, yp, t, hi], down)

    far = (y + 2) % 4

    def got(kind, t):
        spot = {
            0: (o, y, None), 1: (z, ym, None), 2: (z, yp, None), 3: (z, far, lo), 4: (z, far, hi),
            5: (o, ym, None), 6: (o, yp, None), 7: (o, far, lo), 8: (o, far, hi),
        }[kind]
        ref = out.at[spot[0], spot[1], t] if spot[2] is None else out.at[spot[0], spot[1], t, spot[2]]
        cp(kind, t, ref, ref, over).wait_recv()

    for t in range(T):
        send(0, t).start()
        send(1, t).start()
        send(2, t).start()
    for t in range(T):
        out[z, y, t] = own[t]
    for t in range(T):
        got(1, t)
        send(3, t).start()
        got(2, t)
        send(4, t).start()
    for t in range(T + 1):
        if t < T:
            got(0, t)
            send(5, t).start()
            send(6, t).start()
        if t > 0:
            got(5, t - 1)
            send(7, t - 1).start()
            got(6, t - 1)
            send(8, t - 1).start()
    for t in range(T):
        for kind in (3, 4, 7, 8):
            got(kind, t)
    for t in range(T):
        for kind in range(9):
            send(kind, t).wait_send()


def gather(dconv):
    return pl.pallas_call(
        gather_body,
        out_shape=jax.ShapeDtypeStruct((2, 4, T, 32, LP), BF),
        in_specs=[VM], out_specs=VM,
        scratch_shapes=[pltpu.SemaphoreType.DMA((9, T)), pltpu.SemaphoreType.DMA((9, T))],
        compiler_params=params(2), name="gather",
    )(dconv)


def backward_body(dc_ref, pat_ref, w_ref, cw_ref, df_ref, db_ref):
    m = lane_masks()
    for dt in range(3):
        acc = None
        for t in range(2 - dt, T):
            d = dot_nt(pat_ref[t - 2 + dt], dc_ref[:, t].reshape(256, LP))
            acc = d if acc is None else acc + d
        for k in range(9):
            cw_ref[9 * dt + k] = acc[64 * k:64 * (k + 1)].astype(BF)
    cw_ref[27] = jnp.zeros((64, 256), BF)
    for t in range(T):
        acc = None
        for dt in range(3):
            if t + 2 - dt >= T:
                continue
            d = dot(w_ref[dt], dc_ref[:, t + 2 - dt].reshape(256, LP))
            acc = d if acc is None else acc + d
        total = None
        for dw in range(3):
            rows = None
            for dr in range(3):
                k = 3 * dr + dw
                s = row_shift(acc[64 * k:64 * (k + 1)], 1 - dr, m)
                rows = s if rows is None else rows + s
            s = col_shift(rows, 1 - dw, m)
            total = s if total is None else total + s
        for h in range(2):
            df_ref[h, t] = total[32 * h:32 * (h + 1)]
            db_ref[h, t] = total[32 * h:32 * (h + 1)].astype(BF)


def backward(dc, pat, w2):
    return pl.pallas_call(
        backward_body,
        out_shape=(
            jax.ShapeDtypeStruct((4 * G, 64, 256), BF),
            jax.ShapeDtypeStruct((2, T, 32, LP), F32),
            jax.ShapeDtypeStruct((2, T, 32, LP), BF),
        ),
        in_specs=[VM] * 3, out_specs=(VM,) * 3,
        compiler_params=params(), name="backward",
    )(dc, pat, w2)


def exchange_out_body(df_ref, db_ref, act_ref, bt_ref, mask_ref, dst, emb_ref, rx, src, ssem, rsem):
    me, z, y, c = shard_spot()
    barrier([("shard", (me + d) % NS) for d in range(1, NS)])
    pair = rcopy(db_ref.at[1 - c], rx, ssem.at[0], rsem.at[0], "shard", sid(z, y, 1 - c))
    pair.start()
    pair.wait_recv()
    emb = jnp.zeros((32, 32), F32)
    for t in range(T):
        g = (df_ref[c, t] + rx[t].astype(F32)).astype(BF).astype(F32) * mask_ref[t]
        emb = emb + dot_nt(bt_ref[t], g.astype(BF))
        both = jnp.concatenate([act_ref[t].astype(F32), g, jnp.zeros((64, LP), F32)], axis=0)
        src[:, 32 * t:32 * (t + 1), :] = jnp.transpose(both).astype(BF).reshape(NS, 32, 128)
    emb_ref[...] = emb
    sends = []
    for d in range(1, NS):
        peer = (me + d) % NS
        cp = rcopy(src.at[peer], dst.at[me], ssem.at[d], rsem.at[d], "shard", peer)
        cp.start()
        sends.append(cp)
    dst[me] = src[me]
    for d in range(1, NS):
        frm = (me + NS - d) % NS
        rcopy(src.at[frm], dst.at[frm], ssem.at[d], rsem.at[d], "shard", frm).wait_recv()
    for cp in sends:
        cp.wait_send()
    pair.wait_send()


def exchange_out(df, db, act, bt, mask):
    return pl.pallas_call(
        exchange_out_body,
        out_shape=(
            jax.ShapeDtypeStruct((NS, 32 * T, 128), BF),
            jax.ShapeDtypeStruct((32, 32), F32),
        ),
        in_specs=[VM] * 5, out_specs=(VM, VM),
        scratch_shapes=[
            pltpu.VMEM((T, 32, LP), BF),
            pltpu.VMEM((NS, 32 * T, 128), BF),
            pltpu.SemaphoreType.DMA((NS,)),
            pltpu.SemaphoreType.DMA((NS,)),
        ],
        compiler_params=params(3), name="exchange_out",
    )(df, db, act, bt, mask)


def reduce_body(cw, sm, fin, smo, out, rx1, tx2, rx2, sx, rz, xb, zb, ssem, rsem, smss, smrs):
    me, z, y, c = shard_spot()
    dp = lax.axis_index("dp")
    x, l = dp // 4, dp % 4
    xp, xm, far = (x + 1) % 4, (x + 3) % 4, (x + 2) % 4
    fwd, bwd = xp * 4 + l, xm * 4 + l
    pair = sid(z, y, 1 - c)
    lines = [x * 4 + (l + k) % 4 for k in range(1, 4)]
    rings = [((x + k) % 4) * 4 + l for k in range(1, 4)]
    barrier(
        [("dp", p) for p in rings] + [("dp", p) for p in lines]
        + [("shard", (me + d) % NS) for d in range(1, NS)]
    )

    def cp(kind, g, src, dst, peer, axis="dp"):
        return rcopy(src, dst, ssem.at[kind, g], rsem.at[kind, g], axis, peer)

    lo4, hi4 = pl.ds(0, 2), pl.ds(2, 2)

    def send(kind, g):
        if kind == 0:
            return cp(0, g, cw.at[g, far, lo4], rx1.at[0, g], fwd)
        if kind == 1:
            return cp(1, g, cw.at[g, far, hi4], rx1.at[1, g], bwd)
        if kind == 2:
            return cp(2, g, tx2.at[0, g], rx2.at[0, g], fwd)
        if kind == 3:
            return cp(3, g, tx2.at[1, g], rx2.at[1, g], bwd)
        if kind in (4, 5, 6):
            k = kind - 3
            return cp(kind, g, sx.at[g, (l + k) % 4], rz.at[g, k], x * 4 + (l + k) % 4)
        if kind in (7, 8, 9):
            k = kind - 6
            return cp(kind, g, out.at[g, x, l], out.at[g, x, l], x * 4 + (l + k) % 4)
        if kind == 10:
            return cp(10, g, out.at[g, x], out.at[g, x], fwd)
        if kind == 11:
            return cp(11, g, out.at[g, x], out.at[g, x], bwd)
        if kind == 12:
            return cp(12, g, out.at[g, xm, lo4], out.at[g, xm, lo4], fwd)
        if kind == 13:
            return cp(13, g, out.at[g, xp, hi4], out.at[g, xp, hi4], bwd)
        return cp(14, g, out.at[g, :, pl.ds(2 * (1 - c), 2)], fin.at[c, g], pair, "shard")

    def got(kind, g):
        if kind in (0, 1):
            ref = rx1.at[kind, g]
        elif kind in (2, 3):
            ref = rx2.at[kind - 2, g]
        elif kind in (4, 5, 6):
            ref = rz.at[g, kind - 3]
        elif kind in (7, 8, 9):
            ref = out.at[g, x, (l + 10 - kind) % 4]
        elif kind == 10:
            ref = out.at[g, xm]
        elif kind == 11:
            ref = out.at[g, xp]
        elif kind == 12:
            ref = out.at[g, far, lo4]
        elif kind == 13:
            ref = out.at[g, far, hi4]
        else:
            ref = fin.at[1 - c, g]
        cp(kind, g, ref, ref, fwd).wait_recv()

    def s1(g):
        send(0, g).start()
        send(1, g).start()

    def s2(g):
        got(0, g)
        tx2[0, g, 0:2] = (cw[g, xp, 0:2].astype(F32) + rx1[0, g].astype(F32)).astype(BF)
        tx2[0, g, 2:4] = cw[g, xp, 2:4]
        send(2, g).start()
        got(1, g)
        tx2[1, g, 2:4] = (cw[g, xm, 2:4].astype(F32) + rx1[1, g].astype(F32)).astype(BF)
        tx2[1, g, 0:2] = cw[g, xm, 0:2]
        send(3, g).start()

    def s3(g):
        got(2, g)
        got(3, g)
        sx[g] = (cw[g, x].astype(F32) + rx2[0, g].astype(F32) + rx2[1, g].astype(F32)).astype(BF)
        for k in (4, 5, 6):
            send(k, g).start()

    def s4(g):
        for k in (4, 5, 6):
            got(k, g)
        tot = sx[g, l].astype(F32) + rz[g, 1].astype(F32) + rz[g, 2].astype(F32) + rz[g, 3].astype(F32)
        out[g, x, l] = tot.astype(BF)
        for k in (7, 8, 9):
            send(k, g).start()

    def s5(g):
        for k in (7, 8, 9):
            got(k, g)
        send(10, g).start()
        send(11, g).start()

    def s6(g):
        got(10, g)
        send(12, g).start()
        got(11, g)
        send(13, g).start()

    def s7(g):
        got(12, g)
        got(13, g)
        send(14, g).start()
        fin[c, g] = out[g, :, pl.ds(2 * c, 2)]

    def small(kind, k, src, dst, axis, peer):
        return rcopy(src, dst, smss.at[kind, k], smrs.at[kind, k], axis, peer)

    def sm1():
        xb[x] = sm[...]
        for k in range(1, 4):
            small(0, k, sm, xb.at[x], "dp", ((x + k) % 4) * 4 + l).start()

    def sm2():
        for k in range(1, 4):
            small(0, k, sm, xb.at[(x + 4 - k) % 4], "dp", fwd).wait_recv()
        zb[l] = (xb[0] + xb[1]) + (xb[2] + xb[3])
        for k in range(1, 4):
            small(1, k, zb.at[l], zb.at[l], "dp", x * 4 + (l + k) % 4).start()

    def sm3():
        for k in range(1, 4):
            small(1, k, zb.at[l], zb.at[(l + 4 - k) % 4], "dp", fwd).wait_recv()
        smo[me] = (zb[0] + zb[1]) + (zb[2] + zb[3])
        for d in range(1, NS):
            small(2, d, smo.at[me], smo.at[me], "shard", (me + d) % NS).start()

    def sm4():
        for d in range(1, NS):
            small(2, d, smo.at[me], smo.at[(me + NS - d) % NS], "shard", (me + 1) % NS).wait_recv()

    stages = (s1, s2, s3, s4, s5, s6, s7)
    sm1()
    for step in range(G + 6):
        if step == 2:
            sm2()
        if step == 5:
            sm3()
        for k in range(7):
            g = step - k
            if 0 <= g < G:
                stages[k](g)
    sm4()
    for g in range(G):
        got(14, g)
        for kind in range(15):
            send(kind, g).wait_send()
    for k in range(1, 4):
        small(0, k, sm, xb.at[x], "dp", fwd).wait_send()
        small(1, k, zb.at[l], zb.at[l], "dp", fwd).wait_send()
    for d in range(1, NS):
        small(2, d, smo.at[me], smo.at[me], "shard", (me + d) % NS).wait_send()


def reduce(cw, sm):
    piece = (16, 256)
    return pl.pallas_call(
        reduce_body,
        out_shape=(
            jax.ShapeDtypeStruct((2, G, 4, 2) + piece, BF),
            jax.ShapeDtypeStruct((NS, 8, 128), F32),
        ),
        in_specs=[VM, VM], out_specs=(VM, VM),
        scratch_shapes=[
            pltpu.VMEM((G, 4, 4) + piece, BF),
            pltpu.VMEM((2, G, 2) + piece, BF),
            pltpu.VMEM((2, G, 4) + piece, BF),
            pltpu.VMEM((2, G, 4) + piece, BF),
            pltpu.VMEM((G, 4) + piece, BF),
            pltpu.VMEM((G, 4) + piece, BF),
            pltpu.VMEM((4, 8, 128), F32),
            pltpu.VMEM((4, 8, 128), F32),
            pltpu.SemaphoreType.DMA((15, G)),
            pltpu.SemaphoreType.DMA((15, G)),
            pltpu.SemaphoreType.DMA((3, NS)),
            pltpu.SemaphoreType.DMA((3, NS)),
        ],
        compiler_params=params(4), name="reduce",
    )(cw, sm)


def on_device(codes, lengths, hidden, embed, conv_weight, gain, bias, cotangent):
    me = lax.axis_index("shard")
    z, y, c = me // 8, (me // 2) % 4, me % 2
    pos = T * R * WD
    frame_mask = (jnp.arange(T) < lengths[0]).astype(F32)
    powers = 2 ** jnp.arange(CODE_BITS, dtype=jnp.int32)
    bits = (codes[0][..., None] // powers % 2 * 2 - 1).astype(BF)
    embedded = jnp.dot(bits.reshape(pos, CODE_BITS), embed, preferred_element_type=F32)
    cell = jnp.repeat(frame_mask, R * WD)[:, None]
    feats = ((embedded + hidden[0].reshape(pos, 512).astype(F32)) * cell).astype(BF)
    by_chip = feats.reshape(pos, 8, 1, 64).transpose(1, 2, 0, 3)
    by_chip = jnp.broadcast_to(by_chip, (8, 2, pos, 64)).reshape(NS, pos, 64)
    ups = (
        cotangent[0].reshape(T, R, 2, WD, 2, 4, 32)
        .transpose(4, 5, 2, 0, 1, 3, 6).reshape(NS, pos, 32)
    )
    bcast = jnp.broadcast_to(bits.reshape(1, pos, CODE_BITS), (NS, pos, CODE_BITS))
    blocks = jnp.concatenate([by_chip, ups, bcast, jnp.zeros((NS, pos, 14), BF)], axis=2)
    g = exchange_in(blocks)
    w = conv_weight.transpose(1, 0, 2)
    mine = lax.dynamic_slice_in_dim(w, 256 * c, 256, 2)
    give = lax.dynamic_slice_in_dim(w, 256 * (1 - c), 256, 2)
    take = lax.ppermute(give, "shard", [(i, i ^ 1) for i in range(NS)])
    first = jnp.where(c == 0, mine, take)
    second = jnp.where(c == 0, take, mine)
    w2 = jnp.concatenate([first, second], axis=1).reshape(3, 576, 256)
    wt = w2.transpose(0, 2, 1)
    part, ut, bt, pat = forward(g, wt)
    conv = scatter(part.reshape(2, 4, T, 32, LP))
    lo = 256 * c + 32 * (4 * z + y)
    own_gain = lax.dynamic_slice_in_dim(gain, lo, 32).reshape(32, 1)
    own_bias = lax.dynamic_slice_in_dim(bias, lo, 32).reshape(32, 1)
    act, dconv, gb = norm(lengths, conv, ut, own_gain, own_bias)
    dc = gather(dconv)
    cw, df, db = backward(dc.reshape(8, T, 32, LP), pat, w2)
    maskv = jnp.broadcast_to(frame_mask[:, None, None], (T, 1, LP))
    back, emb = exchange_out(df, db, act, bt, maskv)
    sm = jnp.concatenate([emb[:CODE_BITS], gb[:, :2].T, jnp.zeros((12, 32), F32)], axis=0)
    sm = sm.reshape(4, 8, 32).transpose(1, 0, 2).reshape(8, 128)
    fin, smo = reduce(cw.reshape(G, 4, 4, 16, 256), sm)
    grad_conv = (
        fin.reshape(2, 4 * G, 32, 256)[:, :27].transpose(2, 1, 0, 3).reshape(32, 27, 512).astype(F32)
    )
    sums = smo.reshape(NS, 8, 4, 32).transpose(2, 1, 0, 3).reshape(32, NS, 32)
    grad_embed = sums[:CODE_BITS].reshape(CODE_BITS, 512)

    def by_owner(v):
        return v.reshape(2, 4, 2, 32).transpose(2, 0, 1, 3).reshape(512)

    back = back.reshape(2, 4, 2, T, R, WD, 128)
    decoded = (
        back[..., 0:32].transpose(3, 4, 2, 5, 0, 1, 6).reshape(1, T, 2 * R, 2 * WD, 128)
    )
    grad_hidden = (
        back[..., 32:64].transpose(3, 4, 5, 0, 1, 2, 6).reshape(1, T, R, WD, 512)
    )
    return (
        decoded, grad_hidden, grad_conv, grad_embed,
        by_owner(sums[CODE_BITS]), by_owner(sums[CODE_BITS + 1]),
    )


def solution(mesh):
    return jax.shard_map(
        on_device,
        mesh=mesh,
        in_specs=(
            P("dp", None, None, "shard"),
            P("dp"),
            P("dp", None, None, "shard", None),
            P(),
            P("shard", None, None),
            P(),
            P(),
            P("dp", None, None, "shard", None),
        ),
        out_specs=(
            P("dp", None, None, "shard", None),
            P("dp", None, None, "shard", None),
            P("shard", None, None),
            P(),
            P(),
            P(),
        ),
        check_vma=False,
    )
```

time: 615 us -> 206 us (0.33)
  the two profiles are of different devices: /device:TPU:8 before, /device:TPU:1 now
where the time goes in v1:
time: 206 us; the launch traced here: 205 us
  Pallas kernels  177 us (86%)
  local copies, waits for them, and re-layouts  20 us (10%)
  starting transfers between devices  3.29 us (2%)
  other arithmetic  3.01 us (1%)
    pallas_call x1, Pallas kernels, reduce(): pl.pallas_call(reduce_body, out_shape=(jax.ShapeDtypeStruct((2, G, 4, 2)...  62.8 us
    pallas_call x1, Pallas kernels, scatter(): pl.pallas_call(scatter_body, out_shape=jax.ShapeDtypeStruct((T, 32, LP),...  29.3 us
    pallas_call x1, Pallas kernels, exchange_out(): pl.pallas_call(exchange_out_body, out_shape=(jax.ShapeDtypeStruct((NS, 32...  27 us
    pallas_call x1, Pallas kernels, gather(): pl.pallas_call(gather_body, out_shape=jax.ShapeDtypeStruct((2, 4, T, 32,...  22.2 us
    pallas_call x1, Pallas kernels, exchange_in(): pl.pallas_call(a2a_body, out_shape=jax.ShapeDtypeStruct(blocks.shape, blo...  18.9 us
    pallas_call x1, Pallas kernels, backward(): pl.pallas_call(backward_body, out_shape=(jax.ShapeDtypeStruct((4 * G, 64,...  8.22 us
    pallas_call x1, Pallas kernels, forward(): pl.pallas_call(forward_body, out_shape=(jax.ShapeDtypeStruct((8, T, 32, L...  5.66 us
  transfers between devices with their start and end apart: 1, of which 0 were waited for; matrix products, arithmetic and copies ran while one was open for 4% of the time, Pallas kernels for 9%

profile of v1, /device:TPU:1, one launch (start us, length us, event | category | flops | bytes accessed | tf_op | source)
XLA Modules:
  0.0 205.4 jit_solution(2315502091827530253)
XLA Ops:
  0.7 1.0 dynamic-slice_bitcast_fusion
  1.7 3.3 %collective-permute-start = (bf16[27,32,256]{2,1,0:T(8,128)(2,1)S(1)}, bf16[27,32,256]{2,1,0:T(8,128)(2,1)S(1)}, u32[]{:S(2)}, u32[]{:S(2)}) collective-permute-start(bf16[27,32,256]{2,1,0:T(8,128)(2,1)S(1)} %dynamic-slice_bitcast_fusion), channel_id=1, source_target_pairs={{0,1},{1,0},{2,3},{3,2},{4,5},{5,4},{6,7},{7,6},{8,9},{9,8},{10,11... | collective-permute-start | bytes 1327112 | tf_op jit(solution)/shard_map/ppermute | solution.py:678
  5.8 0.8 dynamic-slice_bitcast_fusion.1
  6.6 0.7 copy.29.bias_ref
  7.3 0.7 copy.28.gain_ref
  8.0 0.8 copy.24
  8.9 1.0 reshape.224
  9.9 1.0 fusion.1
  11.9 0.9 fusion.5
  13.0 1.5 maximum_maximum_fusion.src
  14.5 18.9 %exchange_in.1.g_ref = bf16[16,160,128]{2,1,0:T(8,128)(2,1)} custom-call(bf16[16,160,128]{2,1,0:T(8,128)(2,1)} %maximum_maximum_fusion.src), custom_call_target="tpu_custom_call" | custom-call | tf_op jit(solution)/shard_map/exchange_in/pallas_call | solution.py:71
  33.9 1.4 copy.27.wt_ref
  35.3 5.7 %forward.1 = (bf16[8,5,32,512]{3,2,1,0:T(8,128)(2,1)}, bf16[5,32,512]{2,1,0:T(8,128)(2,1)}, bf16[5,32,512]{2,1,0:T(8,128)(2,1)}, bf16[5,576,512]{2,1,0:T(8,128)(2,1)}) custom-call(bf16[16,160,128]{2,1,0:T(8,128)(2,1)} %exchange_in.1.g_ref, bf16[3,256,576]{2,1,0:T(8,128)(2,1)} %copy.27.wt_ref), custom_call_target="tpu_custom_call" | custom-call | tf_op jit(solution)/shard_map/forward/pallas_call | solution.py:147
  40.9 29.3 %scatter.1.conv_ref = f32[5,32,512]{2,1,0:T(8,128)} custom-call(bf16[2,4,5,32,512]{4,3,2,1,0:T(8,128)(2,1)} %bitcast.64), custom_call_target="tpu_custom_call" | custom-call | tf_op jit(solution)/shard_map/scatter/pallas_call | solution.py:224
  70.3 2.3 %norm.1 = (bf16[5,32,512]{2,1,0:T(8,128)(2,1)}, bf16[5,32,512]{2,1,0:T(8,128)(2,1)}, f32[32,128]{1,0:T(8,128)}) custom-call(s32[1]{0:T(128)} %copy.45.len_ref, f32[5,32,512]{2,1,0:T(8,128)} %scatter.1.conv_ref, bf16[5,32,512]{2,1,0:T(8,128)(2,1)} %get-tuple-element.21.ut_ref, f32[32,1]{1,0:T(8,128)} %copy.28.gain_ref, f32[32,1]{1,0:T(8,128)} %copy.29.bias_ref), custom_call_target="tpu_custom_call" | custom-call | tf_op jit(solution)/shard_map/norm/pallas_call | solution.py:285
  72.6 0.8 copy.32
  73.4 22.2 %gather.1 = bf16[2,4,5,32,512]{4,3,2,1,0:T(8,128)(2,1)} custom-call(bf16[5,32,512]{2,1,0:T(8,128)(2,1)} %get-tuple-element.22.own), custom_call_target="tpu_custom_call" | custom-call | tf_op jit(solution)/shard_map/gather/pallas_call | solution.py:369
  95.6 8.2 %backward.1 = (bf16[28,64,256]{2,1,0:T(8,128)(2,1)}, f32[2,5,32,512]{3,2,1,0:T(8,128)}, bf16[2,5,32,512]{3,2,1,0:T(8,128)(2,1)}) custom-call(bf16[8,5,32,512]{3,2,1,0:T(8,128)(2,1)} %bitcast.59, bf16[5,576,512]{2,1,0:T(8,128)(2,1)} %get-tuple-element.23.pat_ref, bf16[3,576,256]{2,1,0:T(8,128)(2,1)} %bitcast.58), custom_call_target="tpu_custom_call" | custom-call | tf_op jit(solution)/shard_map/backward/pallas_call | solution.py:410
  103.8 0.7 broadcast_in_dim.38.mask_ref
  104.5 27.0 %exchange_out.1 = (bf16[16,160,128]{2,1,0:T(8,128)(2,1)}, f32[32,32]{1,0:T(8,128)}) custom-call(f32[2,5,32,512]{3,2,1,0:T(8,128)} %get-tuple-element.24.df_ref, bf16[2,5,32,512]{3,2,1,0:T(8,128)(2,1)} %get-tuple-element.25.db_ref, bf16[5,32,512]{2,1,0:T(8,128)(2,1)} %get-tuple-element.26.act_ref, bf16[5,32,512]{2,1,0:T(8,128)(2,1)} %get-tuple-element.27.bt_ref, ...), custom_call_target="tpu_custom_call" | custom-call | tf_op jit(solution)/shard_map/exchange_out/pallas_call | solution.py:451
  131.5 0.8 slice.26
  132.4 0.7 reshape.217.sm
  133.1 62.8 %reduce.1 = (bf16[2,7,4,2,16,256]{5,4,3,2,1,0:T(8,128)(2,1)}, f32[16,8,128]{2,1,0:T(8,128)}) custom-call(bf16[7,4,4,16,256]{4,3,2,1,0:T(8,128)(2,1)} %bitcast.66, f32[8,128]{1,0:T(8,128)} %reshape.217.sm), custom_call_target="tpu_custom_call" | custom-call | tf_op jit(solution)/shard_map/reduce/pallas_call | solution.py:631
  195.9 1.0 reshape.219
  197.1 0.7 reshape.221
  197.9 0.7 reshape.223
  199.2 0.9 slice_bitcast_fusion
  200.1 0.7 copy.31
  200.8 1.2 reshape.214
  201.9 0.8 copy.30
  202.8 1.0 reshape.213
  204.0 1.4 copy.38
  (41 shorter events, 2.9 us)
Async XLA Ops:
  0.6 9.3 %copy-start = (bf16[18,512]{1,0:T(8,128)(2,1)S(1)}, bf16[18,512]{1,0:T(8,128)(2,1)}, u32[]{:S(2)}) copy-start(bf16[18,512]{1,0:T(8,128)(2,1)} %param.11) | copy-start | bytes 55300
  1.7 31.8 %collective-permute-start = (bf16[27,32,256]{2,1,0:T(8,128)(2,1)S(1)}, bf16[27,32,256]{2,1,0:T(8,128)(2,1)S(1)}, u32[]{:S(2)}, u32[]{:S(2)}) collective-permute-start(bf16[27,32,256]{2,1,0:T(8,128)(2,1)S(1)} %dynamic-slice_bitcast_fusion), channel_id=1, source_target_pairs={{0,1},{1,0},{2,3},{3,2},{4,5},{5,4},{6,7},{7,6},{8,9},{9,8},{10,11... | collective-permute-start | bytes 1327112 | tf_op jit(solution)/shard_map/ppermute | solution.py:678
  8.9 2.3 %copy-start.5 = (bf16[1,5,16,8,128]{4,3,2,1,0:T(8,128)(2,1)S(1)}, bf16[1,5,16,8,128]{4,3,2,1,0:T(8,128)(2,1)}, u32[]{:S(2)}) copy-start(bf16[1,5,16,8,128]{4,3,2,1,0:T(8,128)(2,1)} %param.15) | copy-start | bytes 491524
  14.5 19.0 %copy-start.3 = (bf16[32,27,512]{2,0,1:T(8,128)(2,1)S(1)}, bf16[32,27,512]{2,0,1:T(8,128)(2,1)}, u32[]{:S(2)}) copy-start(bf16[32,27,512]{2,0,1:T(8,128)(2,1)} %param.12) | copy-start | bytes 2654212
  33.9 7.1 %copy-start.1 = (bf16[27,64,256]{2,1,0:T(8,128)(2,1)}, bf16[27,64,256]{2,1,0:T(8,128)(2,1)S(1)}, u32[]{:S(2)}) copy-start(bf16[27,64,256]{2,1,0:T(8,128)(2,1)S(1)} %pad_maximum_fusion) | copy-start | bytes 2654212
  131.5 67.6 %copy-start.2 = (bf16[16,160,128]{2,1,0:T(8,128)(2,1)S(1)}, bf16[16,160,128]{2,1,0:T(8,128)(2,1)}, u32[]{:S(2)}) copy-start(bf16[16,160,128]{2,1,0:T(8,128)(2,1)} %get-tuple-element.28) | copy-start | bytes 1966084
  200.8 3.0 %copy-start.4 = (bf16[2,7,4,2,16,256]{5,4,3,2,1,0:T(8,128)(2,1)S(1)}, bf16[2,7,4,2,16,256]{5,4,3,2,1,0:T(8,128)(2,1)}, u32[]{:S(2)}) copy-start(bf16[2,7,4,2,16,256]{5,4,3,2,1,0:T(8,128)(2,1)} %get-tuple-element.32) | copy-start | bytes 2752516

commit v2 on v0

v2 whole, which is shorter than its diff:
```python
import jax
import jax.numpy as jnp
from jax import lax
from jax.experimental import pallas as pl
from jax.experimental.pallas import tpu as pltpu
from jax.sharding import PartitionSpec as P

BF = jnp.bfloat16
F32 = jnp.float32
CODE_BITS = 18
EPS = 1e-05
T = 5
R = 8
WD = 4
NS = 16
LP = 512
G = 7
MESH = pl.DeviceIdType.MESH
VM = pl.BlockSpec(memory_space=pltpu.VMEM)


def params(cid=None):
    if cid is None:
        return pltpu.CompilerParams(vmem_limit_bytes=60 * 1024 * 1024)
    return pltpu.CompilerParams(
        vmem_limit_bytes=60 * 1024 * 1024, collective_id=cid, has_side_effects=True
    )


def shard_spot():
    me = lax.axis_index("shard")
    return me, me // 8, (me // 2) % 4, me % 2


def sid(z, y, c):
    return z * 8 + y * 2 + c


def rcopy(src, dst, ssem, rsem, axis, peer):
    return pltpu.make_async_remote_copy(
        src_ref=src, dst_ref=dst, send_sem=ssem, recv_sem=rsem,
        device_id={axis: peer}, device_id_type=MESH,
    )


def lane_masks():
    lane = lax.broadcasted_iota(jnp.int32, (1, LP), 1)
    row = (lane // 4) % 8
    col = lane % 4
    return {
        "r0": row >= 1, "r2": row <= 6,
        "c0": col >= 1, "c2": col <= 2,
        "w0": lane % 4 + lane // 32 > 0, "w2": lane % 4 + 4 * (lane // 32) < 63,
    }


def row_shift(x, d, m):
    if d < 0:
        return jnp.where(m["r0"], pltpu.roll(x, 4, 1), 0.0)
    if d > 0:
        return jnp.where(m["r2"], pltpu.roll(x, LP - 4, 1), 0.0)
    return x


def col_shift(x, d, m):
    if d < 0:
        y = jnp.where(m["c0"], pltpu.roll(x, 1, 1), pltpu.roll(x, 29, 1))
        return jnp.where(m["w0"], y, 0.0)
    if d > 0:
        y = jnp.where(m["c2"], pltpu.roll(x, LP - 1, 1), pltpu.roll(x, LP - 29, 1))
        return jnp.where(m["w2"], y, 0.0)
    return x


def dot(a, b):
    return lax.dot_general(a, b, (((1,), (0,)), ((), ())), preferred_element_type=F32)


def dot_nt(a, b):
    return lax.dot_general(a, b, (((1,), (1,)), ((), ())), preferred_element_type=F32)


class Wires:
    def __init__(self, ss, rs):
        self.ss, self.rs, self.ids, self.started = ss, rs, {}, []

    def make(self, name, src, dst, axis, peer):
        n = self.ids.setdefault(name, len(self.ids))
        return rcopy(src, dst, self.ss.at[n], self.rs.at[n], axis, peer)

    def send(self, name, src, dst, axis, peer):
        cp = self.make(name, src, dst, axis, peer)
        cp.start()
        self.started.append(cp)

    def got(self, name, ref):
        self.make(name, ref, ref, "shard", (lax.axis_index("shard") + 1) % NS).wait_recv()

    def finish(self):
        for cp in self.started:
            cp.wait_send()


N_WIRES = 260


def group_sum(x):
    s = jnp.sum(x, axis=1, keepdims=True)
    g = jnp.sum(s.reshape(2, 16, 1), axis=1, keepdims=True)
    return jnp.broadcast_to(g, (2, 16, 1)).reshape(32, 1)


def picks(rows, period):
    ch = lax.broadcasted_iota(jnp.int32, (rows, 128), 0)
    lane = lax.broadcasted_iota(jnp.int32, (rows, 128), 1)
    return (lane % period == ch).astype(F32).astype(BF)


def block_body(
    fe, up, bp, w, gbv, mk,
    dec, gh, fin, smo,
    fsrc, fbuf, u1, u2s, u2, bits, w2s, wts, pat, part, rx1, tx2, rx2, txz, rxz, conv,
    ut, nrm, dpr, act, own, dcs, wacc, cw, df, db, drx, dft, d1s, d1, d2s, d2,
    out, qx1, qt2, qx2, sx, rz, sm, xb, zb, ss, rs,
):
    me, z, y, c = shard_spot()
    dp = lax.axis_index("dp")
    x, l = dp // 4, dp % 4
    o = 1 - z
    yp, ym, far = (y + 1) % 4, (y + 3) % 4, (y + 2) % 4
    up_id, down_id, over, pair = sid(z, yp, c), sid(z, ym, c), sid(o, y, c), sid(z, y, 1 - c)
    xp, xm, xf = (x + 1) % 4, (x + 3) % 4, (x + 2) % 4
    fwd, bwd = xp * 4 + l, xm * 4 + l
    wires = Wires(ss, rs)
    send, got = wires.send, wires.got
    m = lane_masks()
    lane = lax.broadcasted_iota(jnp.int32, (1, 128), 1)
    grp = [(lane // 32 == g).astype(F32) for g in range(4)]
    grpb = [v.astype(BF) for v in grp]
    half = [(lane // 64 == g).astype(F32) for g in range(2)]
    halfb = [v.astype(BF) for v in half]

    barrier_sem = pltpu.get_barrier_semaphore()
    peers = [("shard", (me + d) % NS) for d in range(1, NS)]
    peers += [("dp", ((x + k) % 4) * 4 + l) for k in range(1, 4)]
    peers += [("dp", x * 4 + (l + k) % 4) for k in range(1, 4)]
    for axis, peer in peers:
        pl.semaphore_signal(barrier_sem, inc=1, device_id={axis: peer}, device_id_type=MESH)

    for col in range(4):
        a = fe[0:80, 128 * col:128 * (col + 1)].astype(F32)
        b = fe[80:160, 128 * col:128 * (col + 1)].astype(F32)
        fsrc[2 * col] = (a * half[0] + pltpu.roll(b, 64, 1) * half[1]).astype(BF)
        fsrc[2 * col + 1] = (pltpu.roll(a, 64, 1) * half[0] + b * half[1]).astype(BF)
    chip = 4 * z + y
    fbuf[me] = fsrc[chip]
    u1[2 * z + c] = up[2 * c + z]
    bits[z, y, c] = bp[...]
    pl.semaphore_wait(barrier_sem, len(peers))

    steps = [(0, 1), (0, 3), (1, 0), (0, 2), (1, 1), (1, 3), (1, 2)]
    for dz, dy in steps:
        zz, yy = (z + dz) % 2, (y + dy) % 4
        send(("f", dz, dy), fsrc.at[4 * zz + yy], fbuf.at[me], "shard", sid(zz, yy, c))
    send("fp", fbuf.at[me], fbuf.at[me], "shard", pair)
    send("w", w.at[:, :, pl.ds(pl.multiple_of(256 * (1 - c), 256), 256)], w2s.at[:, c], "shard", pair)
    trio = [(0, 1), (1, 0), (1, 1)]
    for dz, dc in trio:
        zz, cc = (z + dz) % 2, (c + dc) % 2
        send(("u1", dz, dc), up.at[2 * cc + zz], u1.at[2 * z + c], "shard", sid(zz, y, cc))
        send(("b1", dz, dc), bp, bits.at[z, y, c], "shard", sid(zz, y, cc))
    w2s[:, c] = w[:, :, pl.ds(pl.multiple_of(256 * c, 256), 256)]
    got("w", w2s.at[:, 1 - c])
    for dt in range(3):
        wts[dt] = jnp.transpose(w2s[9 * dt:9 * dt + 9].reshape(576, 256).astype(F32)).astype(BF)
    for dz, dy in steps:
        frm = sid((z + dz) % 2, (y + 4 - dy) % 4, c)
        got(("f", dz, dy), fbuf.at[frm])
        send(("fr", dz, dy), fbuf.at[frm], fbuf.at[frm], "shard", pair)
    got("fp", fbuf.at[pair])
    for dz, dy in steps:
        got(("fr", dz, dy), fbuf.at[sid((z + dz) % 2, (y + 4 - dy) % 4, 1 - c)])

    sel64, sel32 = picks(64, 64), picks(32, 32)

    def features(t):
        pieces = []
        for h in range(2):
            p = 32 * t + 16 * h
            k = p // 80
            p = p - 80 * k
            pieces.append(fbuf[:, p:p + 16, :] * halfb[k][None])
        rows = jnp.concatenate(pieces, axis=1).reshape(LP, 128)
        f = dot_nt(sel64, rows)
        for dw in range(3):
            fc = col_shift(f, dw - 1, m)
            for dr in range(3):
                k = 3 * dr + dw
                pat[t, 64 * k:64 * (k + 1), :] = row_shift(fc, dr - 1, m).astype(BF)

    def comp(t):
        features(t)
        acc = None
        for dt in range(3):
            if t - 2 + dt >= 0:
                d = dot(wts[dt], pat[t - 2 + dt])
                acc = d if acc is None else acc + d
        for k in range(8):
            part[k // 4, k % 4, t] = acc[32 * k:32 * (k + 1)].astype(BF)
        send(("s1a", t), part.at[:, far, t, pl.ds(0, 16)], rx1.at[0, t], "shard", up_id)
        send(("s1b", t), part.at[:, far, t, pl.ds(16, 16)], rx1.at[1, t], "shard", down_id)

    def s2(t):
        got(("s1a", t), rx1.at[0, t])
        tx2[0, t, :, 0:16] = (part[:, yp, t, 0:16].astype(F32) + rx1[0, t].astype(F32)).astype(BF)
        tx2[0, t, :, 16:32] = part[:, yp, t, 16:32]
        send(("s2a", t), tx2.at[0, t], rx2.at[0, t], "shard", up_id)
        got(("s1b", t), rx1.at[1, t])
        tx2[1, t, :, 16:32] = (part[:, ym, t, 16:32].astype(F32) + rx1[1, t].astype(F32)).astype(BF)
        tx2[1, t, :, 0:16] = part[:, ym, t, 0:16]
        send(("s2b", t), tx2.at[1, t], rx2.at[1, t], "shard", down_id)

    def s3(t):
        got(("s2a", t), rx2.at[0, t])
        got(("s2b", t), rx2.at[1, t])
        txz[t] = (
            part[o, y, t].astype(F32) + rx2[0, t, o].astype(F32) + rx2[1, t, o].astype(F32)
        ).astype(BF)
        send(("s3", t), txz.at[t], rxz.at[t], "shard", over)
        conv[t] = part[z, y, t].astype(F32) + rx2[0, t, z].astype(F32) + rx2[1, t, z].astype(F32)

    def s4(t):
        got(("s3", t), rxz.at[t])
        conv[t] = conv[t] + rxz[t].astype(F32)

    def u_second():
        for dz, dc in trio:
            zz, cc = (z + dz) % 2, (c + dc) % 2
            got(("u1", dz, dc), u1.at[2 * zz + cc])
            got(("b1", dz, dc), bits.at[zz, y, cc])
        for q in range(4):
            acc = None
            for g in range(4):
                v = u1[g].astype(F32)
                v = v if g == q else pltpu.roll(v, (32 * (g - q)) % 128, 1)
                acc = v * grp[g] if acc is None else acc + v * grp[g]
            u2s[q] = acc.astype(BF)
        for dy in (1, 3, 2):
            yy = (y + dy) % 4
            send(("u2", dy), u2s.at[yy], u2.at[y], "shard", sid(z, yy, c))
            send(("b2", dy), bits.at[:, y], bits.at[:, y], "shard", sid(z, yy, c))
        u2[y] = u2s[y]

    def u_third():
        for dy in (1, 3, 2):
            got(("u2", dy), u2.at[(y + 4 - dy) % 4])
            got(("b2", dy), bits.at[:, (y + 4 - dy) % 4])
        for t in range(T):
            blocks = []
            for s in range(NS):
                blocks.append(u2[(s // 2) % 4, 32 * t:32 * t + 32, :] * grpb[2 * (s // 8) + s % 2])
            ut[t] = dot_nt(sel32, jnp.concatenate(blocks, axis=0))

    def run(events):
        for _, _, f, args in sorted(events, key=lambda e: e[:2]):
            f(*args)

    ev = []
    for t in range(T):
        ev += [
            (1.5 * t, 0, comp, (t,)), (2.6 + 2.1 * t, 1, s2, (t,)),
            (5.2 + 2.1 * t, 2, s3, (t,)), (11.0 + 2.1 * t, 3, s4, (t,)),
        ]
    ev += [(3.1, 9, u_second, ()), (8.0, 9, u_third, ())]
    run(ev)

    count = (mk[0, :, 0:1] + mk[1, :, 0:1] + mk[2, :, 0:1] + mk[3, :, 0:1] + mk[4, :, 0:1]) * float(R * WD * NS * 16)
    s_one = jnp.zeros((32, LP), F32)
    s_two = jnp.zeros((32, LP), F32)
    for t in range(T):
        v = conv[t] * mk[t]
        s_one = s_one + v
        s_two = s_two + conv[t] * v
    mean = group_sum(s_one) / count
    inv = lax.rsqrt(group_sum(s_two) / count - mean * mean + EPS)
    spot = 8 * c + chip
    gain, bias = gbv[0, spot], gbv[1, spot]
    a1 = jnp.zeros((32, LP), F32)
    a2 = jnp.zeros((32, LP), F32)
    for t in range(T):
        n = (conv[t] - mean) * inv
        pre = n * gain + bias
        sg = jax.nn.sigmoid(pre)
        act[t] = pre * sg * mk[t]
        d = ut[t] * mk[t] * sg * (1.0 + pre * (1.0 - sg))
        a1 = a1 + d
        a2 = a2 + d * n
        nrm[t] = n
        dpr[t] = d
    bterm = jnp.sum(a1, axis=1, keepdims=True)
    gterm = jnp.sum(a2, axis=1, keepdims=True)
    t1 = group_sum(gain * bterm) / count
    t2 = group_sum(gain * gterm) / count

    lo, hi = pl.ds(0, 16), pl.ds(16, 16)
    order = [4, 3, 2, 1, 0]
    for t in order:
        own[t] = (inv * (dpr[t] * gain - t1 - nrm[t] * t2) * mk[t]).astype(BF)
        send(("g0", t), own.at[t], dcs.at[z, y, t], "shard", over)
        send(("g1", t), own.at[t], dcs.at[z, y, t], "shard", up_id)
        send(("g2", t), own.at[t], dcs.at[z, y, t], "shard", down_id)
    for t in order:
        dcs[z, y, t] = own[t]

    def first_out(kind, get):
        for t in range(T):
            v = get(t)
            nat = jnp.transpose(jnp.concatenate([v, v, v, v], axis=0))
            for q in range(4):
                acc = None
                for g in range(4):
                    r0 = 32 * sid(g // 2, q, g % 2)
                    piece = nat[r0:r0 + 32] * grp[g]
                    acc = piece if acc is None else acc + piece
                d1s[kind, q, 32 * t:32 * t + 32, :] = acc.astype(BF)
        for dy in (1, 3, 2):
            yy = (y + dy) % 4
            send(("d1", kind, dy), d1s.at[kind, yy], d1.at[kind, y], "shard", sid(z, yy, c))
        d1[kind, y] = d1s[kind, y]

    def second_out(kind, dst):
        for dy in (1, 3, 2):
            got(("d1", kind, dy), d1.at[kind, (y + 4 - dy) % 4])
        for g in range(4):
            acc = None
            for q in range(4):
                v = d1[kind, q].astype(F32)
                v = v if g == q else pltpu.roll(v, (32 * (q - g)) % 128, 1)
                acc = v * grp[q] if acc is None else acc + v * grp[q]
            d2s[kind, g] = acc.astype(BF)
        for dz, dc in trio:
            zz, cc = (z + dz) % 2, (c + dc) % 2
            send(("d2", kind, dz, dc), d2s.at[kind, 2 * zz + cc], dst.at[2 * z + c], "shard", sid(zz, y, cc))
        dst[2 * z + c] = d2s[kind, 2 * z + c]

    def third_out(kind, dst):
        for dz, dc in trio:
            got(("d2", kind, dz, dc), dst.at[2 * ((z + dz) % 2) + (c + dc) % 2])

    def g_near(t):
        got(("g1", t), dcs.at[z, ym, t])
        send(("g3", t), dcs.at[z, ym, t, lo], dcs.at[z, ym, t, lo], "shard", up_id)
        got(("g2", t), dcs.at[z, yp, t])
        send(("g4", t), dcs.at[z, yp, t, hi], dcs.at[z, yp, t, hi], "shard", down_id)

    def g_over(t):
        got(("g0", t), dcs.at[o, y, t])
        send(("g5", t), dcs.at[o, y, t], dcs.at[o, y, t], "shard", up_id)
        send(("g6", t), dcs.at[o, y, t], dcs.at[o, y, t], "shard", down_id)

    def g_far(t):
        got(("g5", t), dcs.at[o, ym, t])
        send(("g7", t), dcs.at[o, ym, t, lo], dcs.at[o, ym, t, lo], "shard", up_id)
        got(("g6", t), dcs.at[o, yp, t])
        send(("g8", t), dcs.at[o, yp, t, hi], dcs.at[o, yp, t, hi], "shard", down_id)

    def g_done(t):
        got(("g3", t), dcs.at[z, far, t, lo])
        got(("g4", t), dcs.at[z, far, t, hi])
        got(("g7", t), dcs.at[o, far, t, lo])
        got(("g8", t), dcs.at[o, far, t, hi])

    def dgrad(t):
        acc = None
        for dt in range(3):
            if t + 2 - dt < T:
                d = dot(w2s[9 * dt:9 * dt + 9].reshape(576, 256), dcs[:, :, t + 2 - dt].reshape(256, LP))
                acc = d if acc is None else acc + d
        total = None
        for dw in range(3):
            rows = None
            for dr in range(3):
                k = 3 * dr + dw
                s = row_shift(acc[64 * k:64 * (k + 1)], 1 - dr, m)
                rows = s if rows is None else rows + s
            s = col_shift(rows, 1 - dw, m)
            total = s if total is None else total + s
        for h in range(2):
            df[h, t] = total[32 * h:32 * (h + 1)]
            db[h, t] = total[32 * h:32 * (h + 1)].astype(BF)
        send(("pair", t), db.at[1 - c, t], drx.at[t], "shard", pair)

    def wgrad(t):
        dct = dcs[:, :, t].reshape(256, LP)
        for dt in range(3):
            if t - 2 + dt < 0:
                continue
            v = dot_nt(pat[t - 2 + dt], dct)
            if t < T - 1:
                v = v + wacc[dt]
            if t == 2 - dt:
                for k in range(9):
                    tap = 9 * dt + k
                    cw[tap // 4, tap % 4] = v[64 * k:64 * (k + 1)].astype(BF).reshape(4, 16, 256)
            else:
                wacc[dt] = v

    def dsum(t):
        got(("pair", t), drx.at[t])
        dft[t] = (df[c, t] + drx[t].astype(F32)).astype(BF).astype(F32) * mk[t]

    lo4, hi4 = pl.ds(0, 2), pl.ds(2, 2)

    def r1(g):
        send(("r0", g), cw.at[g, xf, lo4], qx1.at[0, g], "dp", fwd)
        send(("r1", g), cw.at[g, xf, hi4], qx1.at[1, g], "dp", bwd)

    def r2(g):
        got(("r0", g), qx1.at[0, g])
        qt2[0, g, 0:2] = (cw[g, xp, 0:2].astype(F32) + qx1[0, g].astype(F32)).astype(BF)
        qt2[0, g, 2:4] = cw[g, xp, 2:4]
        send(("r2", g), qt2.at[0, g], qx2.at[0, g], "dp", fwd)
        got(("r1", g), qx1.at[1, g])
        qt2[1, g, 2:4] = (cw[g, xm, 2:4].astype(F32) + qx1[1, g].astype(F32)).astype(BF)
        qt2[1, g, 0:2] = cw[g, xm, 0:2]
        send(("r3", g), qt2.at[1, g], qx2.at[1, g], "dp", bwd)

    def r3(g):
        got(("r2", g), qx2.at[0, g])
        got(("r3", g), qx2.at[1, g])
        sx[g] = (cw[g, x].astype(F32) + qx2[0, g].astype(F32) + qx2[1, g].astype(F32)).astype(BF)
        for k in (3, 2, 1):
            send(("r4", k, g), sx.at[g, (l + k) % 4], rz.at[g, k], "dp", x * 4 + (l + k) % 4)

    def r4(g):
        tot = sx[g, l].astype(F32)
        for k in (1, 2, 3):
            got(("r4", k, g), rz.at[g, k])
            tot = tot + rz[g, k].astype(F32)
        out[g, x, l] = tot.astype(BF)
        for k in (3, 2, 1):
            send(("r7", k, g), out.at[g, x, l], out.at[g, x, l], "dp", x * 4 + (l + k) % 4)

    def r5(g):
        for k in (1, 2, 3):
            got(("r7", k, g), out.at[g, x, (l + 4 - k) % 4])
        send(("r10", g), out.at[g, x], out.at[g, x], "dp", fwd)
        send(("r11", g), out.at[g, x], out.at[g, x], "dp", bwd)

    def r6(g):
        got(("r10", g), out.at[g, xm])
        send(("r12", g), out.at[g, xm, lo4], out.at[g, xm, lo4], "dp", fwd)
        got(("r11", g), out.at[g, xp])
        send(("r13", g), out.at[g, xp, hi4], out.at[g, xp, hi4], "dp", bwd)

    mine = pl.ds(pl.multiple_of(256 * c, 256), 256)
    other = pl.ds(pl.multiple_of(256 * (1 - c), 256), 256)

    def r7(g):
        got(("r12", g), out.at[g, xf, lo4])
        got(("r13", g), out.at[g, xf, hi4])
        send(("r14", g), out.at[g, :, pl.ds(2 * (1 - c), 2)], fin.at[g, :, :, :, mine], "shard", pair)
        fin[g, :, :, :, mine] = out[g, :, pl.ds(2 * c, 2)]

    def m1():
        acc = jnp.zeros((32, 128), F32)
        for t in range(T):
            r0 = 0 if t < 4 else 32
            rows = bits[:, :, :, r0:r0 + 32, :].reshape(LP, 128)
            v = dot(dft[t].astype(BF), rows)
            acc = acc + (v if t % 4 == 0 else pltpu.roll(v, (128 - 32 * (t % 4)) % 128, 1))
        acc = jnp.where(lane < CODE_BITS, acc, 0.0)
        acc = jnp.where(lane == CODE_BITS, gterm, jnp.where(lane == CODE_BITS + 1, bterm, acc))
        e = jnp.transpose(jnp.concatenate([acc, jnp.zeros((96, 128), F32)], axis=0))
        sm[...] = e[0:8] + pltpu.roll(e[8:16], 32, 1) + pltpu.roll(e[16:24], 64, 1)
        xb[x] = sm[...]
        for k in (2, 1, 3):
            send(("m1", k), sm, xb.at[x], "dp", ((x + k) % 4) * 4 + l)

    def m2():
        for k in (1, 2, 3):
            got(("m1", k), xb.at[(x + 4 - k) % 4])
        zb[l] = (xb[0] + xb[1]) + (xb[2] + xb[3])
        for k in (3, 2, 1):
            send(("m2", k), zb.at[l], zb.at[l], "dp", x * 4 + (l + k) % 4)

    def m3():
        for k in (1, 2, 3):
            got(("m2", k), zb.at[(l + 4 - k) % 4])
        smo[me] = (zb[0] + zb[1]) + (zb[2] + zb[3])
        for d in range(1, NS):
            send(("m3", d), smo.at[me], smo.at[me], "shard", (me + d) % NS)

    def m4():
        for d in range(1, NS):
            got(("m3", d), smo.at[(me + NS - d) % NS])

    def last_hidden():
        third_out(1, d2)
        for zz in range(2):
            for h in range(2):
                acc = None
                for g in range(4):
                    v = d2[2 * zz + g % 2].astype(F32)
                    q = 2 * h + g // 2
                    v = v if g == q else pltpu.roll(v, (32 * (g - q)) % 128, 1)
                    acc = v * grp[g] if acc is None else acc + v * grp[g]
                gh[:, 128 * (2 * zz + h):128 * (2 * zz + h + 1)] = acc.astype(BF)

    ev = [(0.1, 0, first_out, (0, lambda t: act[t])), (8.2, 0, second_out, (0, dec))]
    for i, t in enumerate(order):
        ev += [
            (2.4 + 1.1 * i, 1, g_near, (t,)), (5.5 + 1.6 * i, 2, g_over, (t,)),
            (8.5 + 1.6 * i, 3, g_far, (t,)), (11.0 + 2.1 * i, 4, g_done, (t,)),
            (11.0 + 2.1 * i, 5, dgrad, (t,)), (11.0 + 2.1 * i, 6, wgrad, (t,)),
            (13.0 + 2.1 * i, 7, dsum, (t,)),
        ]
    ready = (15.3, 15.4, 17.4, 17.5, 19.5, 19.6, 19.7)
    for g in range(G):
        at = ready[g]
        lag = max(0.0, 15.3 + 1.3 * g - at)
        for off, n, f in ((0.0, 20, r1), (2.2, 21, r2), (4.6, 22, r3), (9.0, 23, r4), (13.5, 24, r5), (16.5, 25, r6), (19.0, 26, r7)):
            ev.append((at + off + (lag if off else 0.0), n, f, (g,)))
    ev += [
        (21.6, 40, m1, ()), (21.7, 41, first_out, (1, lambda t: dft[t])), (25.5, 41, m2, ()), (25.6, 42, second_out, (1, d2)),
        (30.5, 43, m3, ()), (33.0, 44, last_hidden, ()), (37.0, 45, m4, ()), (37.1, 46, third_out, (0, dec)),
    ]
    cw[6, 3] = jnp.zeros((4, 16, 256), BF)
    run(ev)
    for g in range(G):
        got(("r14", g), fin.at[g, :, :, :, other])
    wires.finish()


def block(fe, up, bp, w, gbv, mk):
    v = pltpu.VMEM
    piece = (16, 256)
    return pl.pallas_call(
        block_body,
        out_shape=(
            jax.ShapeDtypeStruct((4, 160, 128), BF),
            jax.ShapeDtypeStruct((160, 512), BF),
            jax.ShapeDtypeStruct((G, 4, 2, 16, 512), BF),
            jax.ShapeDtypeStruct((NS, 8, 128), F32),
        ),
        in_specs=[VM] * 6, out_specs=(VM,) * 4,
        scratch_shapes=[
            v((8, 80, 128), BF), v((NS, 80, 128), BF),
            v((4, 160, 128), BF), v((4, 160, 128), BF), v((4, 160, 128), BF),
            v((2, 4, 2, 64, 128), BF), v((27, 2, 32, 256), BF), v((3, 256, 576), BF),
            v((T, 576, LP), BF), v((2, 4, T, 32, LP), BF),
            v((2, T, 2, 16, LP), BF), v((2, T, 2, 32, LP), BF), v((2, T, 2, 32, LP), BF),
            v((T, 32, LP), BF), v((T, 32, LP), BF), v((T, 32, LP), F32),
            v((T, 32, LP), F32), v((T, 32, LP), F32), v((T, 32, LP), F32), v((T, 32, LP), F32),
            v((T, 32, LP), BF), v((2, 4, T, 32, LP), BF), v((3, 576, 256), F32),
            v((G, 4, 4) + piece, BF),
            v((2, T, 32, LP), F32), v((2, T, 32, LP), BF), v((T, 32, LP), BF), v((T, 32, LP), F32),
            v((2, 4, 160, 128), BF), v((2, 4, 160, 128), BF), v((2, 4, 160, 128), BF), v((4, 160, 128), BF),
            v((G, 4, 4) + piece, BF), v((2, G, 2) + piece, BF), v((2, G, 4) + piece, BF),
            v((2, G, 4) + piece, BF), v((G, 4) + piece, BF), v((G, 4) + piece, BF),
            v((8, 128), F32), v((4, 8, 128), F32), v((4, 8, 128), F32),
            pltpu.SemaphoreType.DMA((N_WIRES,)), pltpu.SemaphoreType.DMA((N_WIRES,)),
        ],
        compiler_params=params(0), name="block",
    )(fe, up, bp, w, gbv, mk)


def on_device(codes, lengths, hidden, embed, conv_weight, gain, bias, cotangent):
    pos = T * R * WD
    frame_mask = (jnp.arange(T) < lengths[0]).astype(F32)
    powers = 2 ** jnp.arange(CODE_BITS, dtype=jnp.int32)
    bits = (codes[0][..., None] // powers % 2 * 2 - 1).astype(BF).reshape(pos, CODE_BITS)
    embedded = jnp.dot(bits, embed, preferred_element_type=F32)
    cell = jnp.repeat(frame_mask, R * WD)[:, None]
    fe = ((embedded + hidden[0].reshape(pos, 512).astype(F32)) * cell).astype(BF)
    up = (
        cotangent[0].reshape(T, R, 2, WD, 2, 128).transpose(2, 4, 0, 1, 3, 5).reshape(4, pos, 128)
    )
    wide = jnp.pad(bits, ((0, 96), (0, 32 - CODE_BITS))).reshape(2, 4, 32, 32)
    bp = wide.transpose(0, 2, 1, 3).reshape(64, 128)
    gbv = jnp.stack([gain, bias]).reshape(2, NS, 32, 1)
    maskv = jnp.broadcast_to(frame_mask[:, None, None], (T, 1, LP))
    dec, gh, fin, smo = block(fe, up, bp, conv_weight.transpose(1, 0, 2), gbv, maskv)
    grad_conv = fin.reshape(4 * G, 32, 512)[:27].astype(F32).transpose(1, 0, 2)
    sums = smo.reshape(NS, 8, 4, 32).transpose(2, 1, 0, 3).reshape(32, NS, 32)
    grad_embed = sums[:CODE_BITS].reshape(CODE_BITS, 512)

    def by_owner(v):
        return v.reshape(2, 4, 2, 32).transpose(2, 0, 1, 3).reshape(512)

    decoded = (
        dec.reshape(2, 2, T, R, WD, 128).transpose(2, 3, 1, 4, 0, 5).reshape(1, T, 2 * R, 2 * WD, 128)
    )
    grad_hidden = gh.reshape(1, T, R, WD, 512)
    return (
        decoded, grad_hidden, grad_conv, grad_embed,
        by_owner(sums[CODE_BITS]), by_owner(sums[CODE_BITS + 1]),
    )


def solution(mesh):
    return jax.shard_map(
        on_device,
        mesh=mesh,
        in_specs=(
            P("dp", None, None, "shard"),
            P("dp"),
            P("dp", None, None, "shard", None),
            P(),
            P("shard", None, None),
            P(),
            P(),
            P("dp", None, None, "shard", None),
        ),
        out_specs=(
            P("dp", None, None, "shard", None),
            P("dp", None, None, "shard", None),
            P("shard", None, None),
            P(),
            P(),
            P(),
        ),
        check_vma=False,
    )
```

time: 615 us -> 135 us (0.22)
  the two profiles are of different devices: /device:TPU:8 before, /device:TPU:1 now
where the time goes in v2:
time: 135 us
  Pallas kernels  116 us (86%)
  local copies, waits for them, and re-layouts  14.5 us (11%)
  other arithmetic  1.82 us (1%)
  between operations  1.39 us (1%)
    pallas_call x1, Pallas kernels, block(): pl.pallas_call(block_body, out_shape=(jax.ShapeDtypeStruct((4, 160, 128),...  116 us

profile of v2, /device:TPU:1, one launch (start us, length us, event | category | flops | bytes accessed | tf_op | source)
XLA Modules:
  0.0 134.9 jit_solution(5955231763087636586)
XLA Ops:
  0.6 0.0 copy-start
  1.3 0.1 broadcast_in_dim.10
  1.4 0.1 mul.78
  1.5 0.8 stack.9
  2.2 0.8 stack.10
  3.0 0.7 broadcast_in_dim.16.mk
  3.7 0.8 copy.25
  4.5 0.1 broadcast_in_dim_squeeze.3
  4.6 0.4 fusion.5
  5.0 0.1 reshape.114
  5.1 0.1 copy.27
  5.2 0.7 reshape.115.bp
  5.9 1.6 %copy.26 = bf16[5,8,2,4,2,128]{5,3,1,0,4,2:T(4,128)(2,1)} copy(bf16[5,8,2,4,2,128]{5,4,3,2,1,0:T(2,128)(2,1)} %bitcast.37) | data formatting | bytes 327680 | tf_op jit(solution)/shard_map/reshape;squeeze | solution.py:577
  7.5 0.9 reshape.125
  8.5 0.0 copy-done
  8.5 1.2 fusion.1.fe
  9.7 1.1 copy.28.gbv
  10.8 116.0 %block.1 = (bf16[4,160,128]{2,1,0:T(8,128)(2,1)}, bf16[160,512]{1,0:T(8,128)(2,1)}, bf16[7,4,2,16,512]{4,3,2,1,0:T(8,128)(2,1)}, f32[16,8,128]{2,1,0:T(8,128)}) custom-call(bf16[160,512]{1,0:T(8,128)(2,1)} %fusion.1.fe, bf16[4,160,128]{2,1,0:T(8,128)(2,1)} %bitcast.35, bf16[64,128]{1,0:T(8,128)(2,1)} %reshape.115.bp, bf16[27,32,512]{2,1,0:T(8,128)(2,1)} %bitcast.31, ...), custom_call_target="tpu_custom_call" | custom-call | tf_op jit(solution)/shard_map/block/pallas_call | solution.py:538
  126.7 0.0 copy-start.1
  126.7 1.8 %copy.29 = bf16[5,8,2,4,2,128]{5,4,3,2,1,0:T(2,128)(2,1)} copy(bf16[5,8,2,4,2,128]{5,3,1,0,2,4:T(4,128)(2,1)} %bitcast.39) | data formatting | bytes 327680 | tf_op jit(solution)/shard_map/transpose | solution.py:592
  128.6 1.6 %reshape.118 = bf16[1,5,8,4,512]{4,3,2,1,0:T(4,128)(2,1)} reshape(bf16[160,512]{1,0:T(8,128)(2,1)} %get-tuple-element.11) | data formatting | bytes 327680 | tf_op jit(solution)/shard_map/reshape | solution.py:594
  130.2 1.0 reshape.120
  131.2 0.2 copy.30
  131.4 0.7 reshape.122
  132.1 0.7 reshape.124
  132.8 0.7 reshape.123
  133.5 0.0 copy-done.1
  133.5 1.4 %convert_bitcast_fusion = f32[32,27,512]{2,0,1:T(8,128)} fusion(bf16[28,32,512]{2,1,0:T(8,128)(2,1)S(1)} %bitcast.32), kind=kLoop, calls=%fused_computation | loop fusion | flops 442368 | bytes 2654208 | tf_op jit(solution)/shard_map/transpose | solution.py:584
  (9 shorter events, 0.1 us)
Async XLA Ops:
  0.6 7.8 %copy-start = (bf16[18,512]{1,0:T(8,128)(2,1)S(1)}, bf16[18,512]{1,0:T(8,128)(2,1)}, u32[]{:S(2)}) copy-start(bf16[18,512]{1,0:T(8,128)(2,1)} %param.11) | copy-start | bytes 55300
  126.7 6.7 %copy-start.1 = (bf16[7,4,2,16,512]{4,3,2,1,0:T(8,128)(2,1)S(1)}, bf16[7,4,2,16,512]{4,3,2,1,0:T(8,128)(2,1)}, u32[]{:S(2)}) copy-start(bf16[7,4,2,16,512]{4,3,2,1,0:T(8,128)(2,1)} %get-tuple-element.12) | copy-start | bytes 2752516

commit v3 on v2

--- a/solution.py
+++ b/solution.py
@@ -116,11 +116,18 @@
     return (lane % period == ch).astype(F32).astype(BF)
 
 
+def placing(way):
+    dst = lax.broadcasted_iota(jnp.int32, (128, 128), way)
+    src = lax.broadcasted_iota(jnp.int32, (128, 128), 1 - way)
+    a, b, r, w = dst // 64, (dst // 32) % 2, (dst // 4) % 8, dst % 4
+    return (src == 16 * r + 8 * a + 2 * w + b).astype(F32).astype(BF)
+
+
 def block_body(
-    fe, up, bp, w, gbv, mk,
-    dec, gh, fin, smo,
-    fsrc, fbuf, u1, u2s, u2, bits, w2s, wts, pat, part, rx1, tx2, rx2, txz, rxz, conv,
-    ut, nrm, dpr, act, own, dcs, wacc, cw, df, db, drx, dft, d1s, d1, d2s, d2,
+    length_ref, ci, hid, emb_ref, w, gain_ref, bias_ref, cot,
+    dec, gho, fin, smo,
+    epad, fe, up, gcol, cbuf, fsrc, fbuf, u1, u2s, u2, w2s, wts, pat, part, rx1, tx2, rx2, txz, rxz, conv,
+    ut, nrm, dpr, act, own, dcs, wacc, cw, df, db, drx, dft, d1s, d1, d2s,
     out, qx1, qt2, qx2, sx, rz, sm, xb, zb, ss, rs,
 ):
     me, z, y, c = shard_spot()
@@ -147,6 +154,28 @@
     for axis, peer in peers:
         pl.semaphore_signal(barrier_sem, inc=1, device_id={axis: peer}, device_id_type=MESH)
 
+    length = length_ref[0]
+    mk = [jnp.where(t < length, 1.0, 0.0) for t in range(T)]
+    bit = lax.broadcasted_iota(jnp.int32, (128, 128), 0)
+    epad[...] = jnp.zeros((128, 512), BF)
+    epad[0:CODE_BITS] = emb_ref[...]
+    for h in range(2):
+        code = jnp.broadcast_to(ci[h:h + 1, :], (128, 128))
+        signs = jnp.where(bit < CODE_BITS, (lax.shift_right_logical(code, jnp.minimum(bit, 31)) & 1) * 2 - 1, 0)
+        nat = dot(jnp.transpose(signs.astype(F32)).astype(BF), epad[...])
+        for t in range(4 * h, min(T, 4 * h + 4)):
+            r0 = 32 * (t - 4 * h)
+            fe[32 * t:32 * t + 32] = (
+                (nat[r0:r0 + 32] + hid[32 * t:32 * t + 32].astype(F32)) * mk[t]
+            ).astype(BF)
+    place = placing(0)
+    for t in range(T):
+        v = dot(place, cot[128 * t:128 * t + 128]).astype(BF)
+        for q in range(4):
+            up[q, 32 * t:32 * t + 32] = v[32 * q:32 * q + 32]
+    for k, ref in enumerate((gain_ref, bias_ref)):
+        gcol[k] = jnp.transpose(jnp.broadcast_to(ref[pl.ds(2 * c + z, 1), :], (128, 128)))
+
     for col in range(4):
         a = fe[0:80, 128 * col:128 * (col + 1)].astype(F32)
         b = fe[80:160, 128 * col:128 * (col + 1)].astype(F32)
@@ -155,7 +184,7 @@
     chip = 4 * z + y
     fbuf[me] = fsrc[chip]
     u1[2 * z + c] = up[2 * c + z]
-    bits[z, y, c] = bp[...]
+    cbuf[me] = ci[...]
     pl.semaphore_wait(barrier_sem, len(peers))
 
     steps = [(0, 1), (0, 3), (1, 0), (0, 2), (1, 1), (1, 3), (1, 2)]
@@ -164,11 +193,6 @@
         send(("f", dz, dy), fsrc.at[4 * zz + yy], fbuf.at[me], "shard", sid(zz, yy, c))
     send("fp", fbuf.at[me], fbuf.at[me], "shard", pair)
     send("w", w.at[:, :, pl.ds(pl.multiple_of(256 * (1 - c), 256), 256)], w2s.at[:, c], "shard", pair)
-    trio = [(0, 1), (1, 0), (1, 1)]
-    for dz, dc in trio:
-        zz, cc = (z + dz) % 2, (c + dc) % 2
-        send(("u1", dz, dc), up.at[2 * cc + zz], u1.at[2 * z + c], "shard", sid(zz, y, cc))
-        send(("b1", dz, dc), bp, bits.at[z, y, c], "shard", sid(zz, y, cc))
     w2s[:, c] = w[:, :, pl.ds(pl.multiple_of(256 * c, 256), 256)]
     got("w", w2s.at[:, 1 - c])
     for dt in range(3):
@@ -178,6 +202,12 @@
         got(("f", dz, dy), fbuf.at[frm])
         send(("fr", dz, dy), fbuf.at[frm], fbuf.at[frm], "shard", pair)
     got("fp", fbuf.at[pair])
+    trio = [(0, 1), (1, 0), (1, 1)]
+    for dz, dc in trio:
+        zz, cc = (z + dz) % 2, (c + dc) % 2
+        send(("u1", dz, dc), up.at[2 * cc + zz], u1.at[2 * z + c], "shard", sid(zz, y, cc))
+    for d in range(1, NS):
+        send(("b", d), ci, cbuf.at[me], "shard", (me + d) % NS)
     for dz, dy in steps:
         got(("fr", dz, dy), fbuf.at[sid((z + dz) % 2, (y + 4 - dy) % 4, 1 - c)])
 
@@ -237,7 +267,6 @@
         for dz, dc in trio:
             zz, cc = (z + dz) % 2, (c + dc) % 2
             got(("u1", dz, dc), u1.at[2 * zz + cc])
-            got(("b1", dz, dc), bits.at[zz, y, cc])
         for q in range(4):
             acc = None
             for g in range(4):
@@ -248,13 +277,11 @@
         for dy in (1, 3, 2):
             yy = (y + dy) % 4
             send(("u2", dy), u2s.at[yy], u2.at[y], "shard", sid(z, yy, c))
-            send(("b2", dy), bits.at[:, y], bits.at[:, y], "shard", sid(z, yy, c))
         u2[y] = u2s[y]
 
     def u_third():
         for dy in (1, 3, 2):
             got(("u2", dy), u2.at[(y + 4 - dy) % 4])
-            got(("b2", dy), bits.at[:, (y + 4 - dy) % 4])
         for t in range(T):
             blocks = []
             for s in range(NS):
@@ -271,10 +298,10 @@
             (1.5 * t, 0, comp, (t,)), (2.6 + 2.1 * t, 1, s2, (t,)),
             (5.2 + 2.1 * t, 2, s3, (t,)), (11.0 + 2.1 * t, 3, s4, (t,)),
         ]
-    ev += [(3.1, 9, u_second, ()), (8.0, 9, u_third, ())]
+    ev += [(7.0, 9, u_second, ()), (14.5, 9, u_third, ())]
     run(ev)
 
-    count = (mk[0, :, 0:1] + mk[1, :, 0:1] + mk[2, :, 0:1] + mk[3, :, 0:1] + mk[4, :, 0:1]) * float(R * WD * NS * 16)
+    count = length.astype(F32) * float(R * WD * NS * 16)
     s_one = jnp.zeros((32, LP), F32)
     s_two = jnp.zeros((32, LP), F32)
     for t in range(T):
@@ -283,8 +310,8 @@
         s_two = s_two + conv[t] * v
     mean = group_sum(s_one) / count
     inv = lax.rsqrt(group_sum(s_two) / count - mean * mean + EPS)
-    spot = 8 * c + chip
-    gain, bias = gbv[0, spot], gbv[1, spot]
+    mine32 = pl.ds(pl.multiple_of(32 * y, 32), 32)
+    gain, bias = gcol[0, mine32, 0:1], gcol[1, mine32, 0:1]
     a1 = jnp.zeros((32, LP), F32)
     a2 = jnp.zeros((32, LP), F32)
     for t in range(T):
@@ -312,8 +339,8 @@
     for t in order:
         dcs[z, y, t] = own[t]
 
-    def first_out(kind, get):
-        for t in range(T):
+    def first_out(kind, get, t0, t1):
+        for t in range(t0, t1):
             v = get(t)
             nat = jnp.transpose(jnp.concatenate([v, v, v, v], axis=0))
             for q in range(4):
@@ -325,27 +352,35 @@
                 d1s[kind, q, 32 * t:32 * t + 32, :] = acc.astype(BF)
         for dy in (1, 3, 2):
             yy = (y + dy) % 4
-            send(("d1", kind, dy), d1s.at[kind, yy], d1.at[kind, y], "shard", sid(z, yy, c))
-        d1[kind, y] = d1s[kind, y]
-
-    def second_out(kind, dst):
+            part_of = pl.ds(32 * t0, 32 * (t1 - t0))
+            send(
+                ("d1", kind, t0, dy), d1s.at[kind, yy, part_of], d1.at[kind, y, part_of], "shard", sid(z, yy, c)
+            )
+        d1[kind, y, 32 * t0:32 * t1] = d1s[kind, y, 32 * t0:32 * t1]
+
+    def second_out(kind, dst, t0, t1):
+        part_of = pl.ds(32 * t0, 32 * (t1 - t0))
         for dy in (1, 3, 2):
-            got(("d1", kind, dy), d1.at[kind, (y + 4 - dy) % 4])
+            got(("d1", kind, t0, dy), d1.at[kind, (y + 4 - dy) % 4, part_of])
         for g in range(4):
             acc = None
             for q in range(4):
-                v = d1[kind, q].astype(F32)
+                v = d1[kind, q, 32 * t0:32 * t1].astype(F32)
                 v = v if g == q else pltpu.roll(v, (32 * (q - g)) % 128, 1)
                 acc = v * grp[q] if acc is None else acc + v * grp[q]
-            d2s[kind, g] = acc.astype(BF)
+            d2s[kind, g, 32 * t0:32 * t1] = acc.astype(BF)
         for dz, dc in trio:
             zz, cc = (z + dz) % 2, (c + dc) % 2
-            send(("d2", kind, dz, dc), d2s.at[kind, 2 * zz + cc], dst.at[2 * z + c], "shard", sid(zz, y, cc))
-        dst[2 * z + c] = d2s[kind, 2 * z + c]
-
-    def third_out(kind, dst):
+            send(
+                ("d2", kind, t0, dz, dc), d2s.at[kind, 2 * zz + cc, part_of], dst.at[2 * z + c, part_of],
+                "shard", sid(zz, y, cc),
+            )
+        dst[2 * z + c, 32 * t0:32 * t1] = d2s[kind, 2 * z + c, 32 * t0:32 * t1]
+
+    def third_out(kind, dst, t0, t1):
+        part_of = pl.ds(32 * t0, 32 * (t1 - t0))
         for dz, dc in trio:
-            got(("d2", kind, dz, dc), dst.at[2 * ((z + dz) % 2) + (c + dc) % 2])
+            got(("d2", kind, t0, dz, dc), dst.at[2 * ((z + dz) % 2) + (c + dc) % 2, part_of])
 
     def g_near(t):
         got(("g1", t), dcs.at[z, ym, t])
@@ -463,16 +498,30 @@
         fin[g, :, :, :, mine] = out[g, :, pl.ds(2 * c, 2)]
 
     def m1():
+        for d in range(1, NS):
+            got(("b", d), cbuf.at[(me + NS - d) % NS])
+        grpi = [(lane // 32 == g).astype(jnp.int32) for g in range(4)]
+        bit32 = lax.broadcasted_iota(jnp.int32, (32, LP), 0)
         acc = jnp.zeros((32, 128), F32)
-        for t in range(T):
-            r0 = 0 if t < 4 else 32
-            rows = bits[:, :, :, r0:r0 + 32, :].reshape(LP, 128)
-            v = dot(dft[t].astype(BF), rows)
-            acc = acc + (v if t % 4 == 0 else pltpu.roll(v, (128 - 32 * (t % 4)) % 128, 1))
-        acc = jnp.where(lane < CODE_BITS, acc, 0.0)
-        acc = jnp.where(lane == CODE_BITS, gterm, jnp.where(lane == CODE_BITS + 1, bterm, acc))
-        e = jnp.transpose(jnp.concatenate([acc, jnp.zeros((96, 128), F32)], axis=0))
-        sm[...] = e[0:8] + pltpu.roll(e[8:16], 32, 1) + pltpu.roll(e[16:24], 64, 1)
+        for f in range(4):
+            cols = []
+            for q in range(4):
+                v = None
+                for j in range(4):
+                    r = cbuf[4 * q + j]
+                    r = r if j == f else pltpu.roll(r, (32 * (j - f)) % 128, 1)
+                    v = r * grpi[j] if v is None else v + r * grpi[j]
+                cols.append(v)
+            for t in ((0, 4) if f == 0 else (f,)):
+                code = jnp.concatenate([v[t // 4:t // 4 + 1] for v in cols], axis=1)
+                code = jnp.broadcast_to(code, (32, LP))
+                signs = jnp.where(bit32 < CODE_BITS, (lax.shift_right_logical(code, bit32) & 1) * 2 - 1, 0)
+                rhs = jnp.concatenate([dft[t], jnp.zeros((96, LP), F32)], axis=0).astype(BF)
+                acc = acc + dot_nt(signs.astype(F32).astype(BF), rhs)
+        cols = jnp.where(lane == 0, gterm, jnp.where(lane == 1, bterm, 0.0))
+        gb = jnp.transpose(jnp.concatenate([cols, jnp.zeros((96, 128), F32)], axis=0))
+        e = acc[16:24] + pltpu.roll(gb[0:8], 2, 0)
+        sm[...] = acc[0:8] + pltpu.roll(acc[8:16], 32, 1) + pltpu.roll(e, 64, 1)
         xb[x] = sm[...]
         for k in (2, 1, 3):
             send(("m1", k), sm, xb.at[x], "dp", ((x + k) % 4) * 4 + l)
@@ -495,35 +544,27 @@
         for d in range(1, NS):
             got(("m3", d), smo.at[(me + NS - d) % NS])
 
-    def last_hidden():
-        third_out(1, d2)
-        for zz in range(2):
-            for h in range(2):
-                acc = None
-                for g in range(4):
-                    v = d2[2 * zz + g % 2].astype(F32)
-                    q = 2 * h + g // 2
-                    v = v if g == q else pltpu.roll(v, (32 * (g - q)) % 128, 1)
-                    acc = v * grp[g] if acc is None else acc + v * grp[g]
-                gh[:, 128 * (2 * zz + h):128 * (2 * zz + h + 1)] = acc.astype(BF)
-
-    ev = [(0.1, 0, first_out, (0, lambda t: act[t])), (8.2, 0, second_out, (0, dec))]
+    ev = [(0.1, 0, first_out, (0, lambda t: act[t], 0, T)), (8.2, 0, second_out, (0, dec, 0, T))]
     for i, t in enumerate(order):
         ev += [
             (2.4 + 1.1 * i, 1, g_near, (t,)), (5.5 + 1.6 * i, 2, g_over, (t,)),
             (8.5 + 1.6 * i, 3, g_far, (t,)), (11.0 + 2.1 * i, 4, g_done, (t,)),
-            (11.0 + 2.1 * i, 5, dgrad, (t,)), (11.0 + 2.1 * i, 6, wgrad, (t,)),
-            (13.0 + 2.1 * i, 7, dsum, (t,)),
+            (11.0 + 2.1 * i, 5, wgrad, (t,)), (11.1 + 2.1 * i, 30, dgrad, (t,)),
+            (13.2 + 2.1 * i, 7, dsum, (t,)),
         ]
-    ready = (15.3, 15.4, 17.4, 17.5, 19.5, 19.6, 19.7)
+    ready = (15.22, 15.24, 17.32, 17.34, 19.42, 19.44, 19.46)
     for g in range(G):
         at = ready[g]
-        lag = max(0.0, 15.3 + 1.3 * g - at)
-        for off, n, f in ((0.0, 20, r1), (2.2, 21, r2), (4.6, 22, r3), (9.0, 23, r4), (13.5, 24, r5), (16.5, 25, r6), (19.0, 26, r7)):
+        lag = max(0.0, 15.3 + 1.0 * g - at)
+        for off, n, f in ((0.0, 20, r1), (2.2, 21, r2), (4.6, 22, r3), (9.0, 23, r4), (13.0, 24, r5), (15.5, 25, r6), (18.0, 26, r7)):
             ev.append((at + off + (lag if off else 0.0), n, f, (g,)))
+    get = lambda t: dft[t]
     ev += [
-        (21.6, 40, m1, ()), (21.7, 41, first_out, (1, lambda t: dft[t])), (25.5, 41, m2, ()), (25.6, 42, second_out, (1, d2)),
-        (30.5, 43, m3, ()), (33.0, 44, last_hidden, ()), (37.0, 45, m4, ()), (37.1, 46, third_out, (0, dec)),
+        (17.5, 30, first_out, (1, get, 2, T)), (20.6, 31, second_out, (1, gho, 2, T)),
+        (21.7, 40, first_out, (1, get, 0, 2)), (21.8, 41, m1, ()),
+        (25.3, 41, second_out, (1, gho, 0, 2)), (26.0, 42, m2, ()), (31.0, 43, m3, ()),
+        (37.0, 45, m4, ()), (37.1, 46, third_out, (0, dec, 0, T)),
+        (37.2, 47, third_out, (1, gho, 2, T)), (37.3, 48, third_out, (1, gho, 0, 2)),
     ]
     cw[6, 3] = jnp.zeros((4, 16, 256), BF)
     run(ev)
@@ -532,22 +573,24 @@
     wires.finish()
 
 
-def block(fe, up, bp, w, gbv, mk):
+def block(lengths, ci, hid, emb, w, gain, bias, cot):
     v = pltpu.VMEM
     piece = (16, 256)
     return pl.pallas_call(
         block_body,
         out_shape=(
             jax.ShapeDtypeStruct((4, 160, 128), BF),
-            jax.ShapeDtypeStruct((160, 512), BF),
+            jax.ShapeDtypeStruct((4, 160, 128), BF),
             jax.ShapeDtypeStruct((G, 4, 2, 16, 512), BF),
             jax.ShapeDtypeStruct((NS, 8, 128), F32),
         ),
-        in_specs=[VM] * 6, out_specs=(VM,) * 4,
+        in_specs=[pl.BlockSpec(memory_space=pltpu.SMEM)] + [VM] * 7, out_specs=(VM,) * 4,
         scratch_shapes=[
+            v((128, 512), BF), v((160, 512), BF), v((4, 160, 128), BF), v((2, 128, 128), F32),
+            v((NS, 8, 128), jnp.int32),
             v((8, 80, 128), BF), v((NS, 80, 128), BF),
             v((4, 160, 128), BF), v((4, 160, 128), BF), v((4, 160, 128), BF),
-            v((2, 4, 2, 64, 128), BF), v((27, 2, 32, 256), BF), v((3, 256, 576), BF),
+            v((27, 2, 32, 256), BF), v((3, 256, 576), BF),
             v((T, 576, LP), BF), v((2, 4, T, 32, LP), BF),
             v((2, T, 2, 16, LP), BF), v((2, T, 2, 32, LP), BF), v((2, T, 2, 32, LP), BF),
             v((T, 32, LP), BF), v((T, 32, LP), BF), v((T, 32, LP), F32),
@@ -555,46 +598,74 @@
             v((T, 32, LP), BF), v((2, 4, T, 32, LP), BF), v((3, 576, 256), F32),
             v((G, 4, 4) + piece, BF),
             v((2, T, 32, LP), F32), v((2, T, 32, LP), BF), v((T, 32, LP), BF), v((T, 32, LP), F32),
-            v((2, 4, 160, 128), BF), v((2, 4, 160, 128), BF), v((2, 4, 160, 128), BF), v((4, 160, 128), BF),
+            v((2, 4, 160, 128), BF), v((2, 4, 160, 128), BF), v((2, 4, 160, 128), BF),
             v((G, 4, 4) + piece, BF), v((2, G, 2) + piece, BF), v((2, G, 4) + piece, BF),
             v((2, G, 4) + piece, BF), v((G, 4) + piece, BF), v((G, 4) + piece, BF),
             v((8, 128), F32), v((4, 8, 128), F32), v((4, 8, 128), F32),
             pltpu.SemaphoreType.DMA((N_WIRES,)), pltpu.SemaphoreType.DMA((N_WIRES,)),
         ],
         compiler_params=params(0), name="block",
-    )(fe, up, bp, w, gbv, mk)
+    )(lengths, ci, hid, emb, w, gain, bias, cot)
+
+
+def outputs_body(dec, gho, fin, smo, dec_o, gh_o, gc_o, ge_o, gg_o, gb_o):
+    lane = lax.broadcasted_iota(jnp.int32, (1, 128), 1)
+    grp = [(lane // 32 == g).astype(F32) for g in range(4)]
+
+    def gathered(parts):
+        acc = None
+        for g, (v, q) in enumerate(parts):
+            v = v.astype(F32)
+            v = v if g == q else pltpu.roll(v, (32 * (g - q)) % 128, 1)
+            acc = v * grp[g] if acc is None else acc + v * grp[g]
+        return acc
+
+    for tap in range(27):
+        gc_o[tap] = fin[tap // 4, tap % 4].reshape(32, 512).astype(F32)
+    back = placing(1)
+    for t in range(T):
+        rows = slice(32 * t, 32 * t + 32)
+        v = jnp.concatenate([dec[0, rows], dec[2, rows], dec[1, rows], dec[3, rows]], axis=0)
+        dec_o[128 * t:128 * t + 128] = dot(back, v).astype(BF)
+    for zz in range(2):
+        for h in range(2):
+            col = 2 * zz + h
+            gh_o[:, 128 * col:128 * (col + 1)] = gathered(
+                [(gho[2 * zz + g % 2], 2 * h + g // 2) for g in range(4)]
+            ).astype(BF)
+    for q in range(4):
+        cols = slice(128 * q, 128 * (q + 1))
+        for a in range(3):
+            v = gathered([(smo[4 * q + j], a) for j in range(4)])
+            n = min(8, CODE_BITS - 8 * a)
+            ge_o[8 * a:8 * a + n, cols] = v[0:n]
+        v = gathered([(smo[sid(q % 2, j, q // 2)], 2) for j in range(4)])
+        gg_o[q:q + 1] = v[2:3]
+        gb_o[q:q + 1] = v[3:4]
+
+
+def outputs(dec, gho, fin, smo):
+    s = jax.ShapeDtypeStruct
+    return pl.pallas_call(
+        outputs_body,
+        out_shape=(
+            s((640, 128), BF), s((160, 512), BF), s((27, 32, 512), F32), s((CODE_BITS, 512), F32),
+            s((4, 128), F32), s((4, 128), F32),
+        ),
+        in_specs=[VM] * 4, out_specs=(VM,) * 6, compiler_params=params(), name="outputs",
+    )(dec, gho, fin, smo)
 
 
 def on_device(codes, lengths, hidden, embed, conv_weight, gain, bias, cotangent):
-    pos = T * R * WD
-    frame_mask = (jnp.arange(T) < lengths[0]).astype(F32)
-    powers = 2 ** jnp.arange(CODE_BITS, dtype=jnp.int32)
-    bits = (codes[0][..., None] // powers % 2 * 2 - 1).astype(BF).reshape(pos, CODE_BITS)
-    embedded = jnp.dot(bits, embed, preferred_element_type=F32)
-    cell = jnp.repeat(frame_mask, R * WD)[:, None]
-    fe = ((embedded + hidden[0].reshape(pos, 512).astype(F32)) * cell).astype(BF)
-    up = (
-        cotangent[0].reshape(T, R, 2, WD, 2, 128).transpose(2, 4, 0, 1, 3, 5).reshape(4, pos, 128)
+    ci = jnp.pad(codes.reshape(160), (0, 864)).reshape(8, 128)
+    raw = block(
+        lengths, ci, hidden.reshape(160, 512), embed, conv_weight.transpose(1, 0, 2),
+        gain.reshape(4, 128), bias.reshape(4, 128), cotangent.reshape(640, 128),
     )
-    wide = jnp.pad(bits, ((0, 96), (0, 32 - CODE_BITS))).reshape(2, 4, 32, 32)
-    bp = wide.transpose(0, 2, 1, 3).reshape(64, 128)
-    gbv = jnp.stack([gain, bias]).reshape(2, NS, 32, 1)
-    maskv = jnp.broadcast_to(frame_mask[:, None, None], (T, 1, LP))
-    dec, gh, fin, smo = block(fe, up, bp, conv_weight.transpose(1, 0, 2), gbv, maskv)
-    grad_conv = fin.reshape(4 * G, 32, 512)[:27].astype(F32).transpose(1, 0, 2)
-    sums = smo.reshape(NS, 8, 4, 32).transpose(2, 1, 0, 3).reshape(32, NS, 32)
-    grad_embed = sums[:CODE_BITS].reshape(CODE_BITS, 512)
-
-    def by_owner(v):
-        return v.reshape(2, 4, 2, 32).transpose(2, 0, 1, 3).reshape(512)
-
-    decoded = (
-        dec.reshape(2, 2, T, R, WD, 128).transpose(2, 3, 1, 4, 0, 5).reshape(1, T, 2 * R, 2 * WD, 128)
-    )
-    grad_hidden = gh.reshape(1, T, R, WD, 512)
+    dec, gh, gc, ge, gg, gb = outputs(*raw)
     return (
-        decoded, grad_hidden, grad_conv, grad_embed,
-        by_owner(sums[CODE_BITS]), by_owner(sums[CODE_BITS + 1]),
+        dec.reshape(1, T, 2 * R, 2 * WD, 128), gh.reshape(1, T, R, WD, 512), gc.transpose(1, 0, 2), ge,
+        gg.reshape(512), gb.reshape(512),
     )
 
 

time: 135 us -> 116 us (0.86)
  local copies, waits for them, and re-layouts: 14.5 us -> 4.75 us
  Pallas kernels: 116 us -> 110 us
  other arithmetic: 1.82 us -> 0 us
    pallas_call x1, Pallas kernels: 116 us -> 107 us  [block(): pl.pallas_call(block_body, out_shape=(jax.ShapeDtypeStruct((4, 160, 128),...]
    another operation x7 -> x0, local copies, waits for them, and re-layouts: 4.31 us -> none  [the longest x3 2.58 us: on_device(): gbv = jnp.stack([gain, bias]).reshape(2, NS, 32, 1)]
    pallas_call x0 -> x1, Pallas kernels: none -> 2.94 us  [outputs(): pl.pallas_call(outputs_body, out_shape=(s((640, 128), BF), s((160, 512),...]
    transpose x2 -> x0, local copies, waits for them, and re-layouts: 1.96 us -> none  [the longest x1 1.83 us: on_device(): dec.reshape(2, 2, T, R, WD, 128).transpose(2, 3, 1, 4, 0, 5)]
    reshape x8 -> x4, local copies, waits for them, and re-layouts: 5.65 us -> 3.95 us  [the longest x1 1.63 us: on_device(): gh.reshape(1, T, R, WD, 512)]
    transpose x1 -> x0, other arithmetic: 1.44 us -> none  [on_device(): grad_conv = fin.reshape(4 * G, 32, 512)[:27].astype(F32).transpose(1, 0, 2)]
where the time goes in v3:
time: 116 us
  Pallas kernels  110 us (95%)
  local copies, waits for them, and re-layouts  4.75 us (4%)
  between operations  1.29 us (1%)
    pallas_call x1, Pallas kernels, block(): pl.pallas_call(block_body, out_shape=(jax.ShapeDtypeStruct((4, 160, 128),...  107 us
    pallas_call x1, Pallas kernels, outputs(): pl.pallas_call(outputs_body, out_shape=(s((640, 128), BF), s((160, 512),...  2.94 us

profile of v3, /device:TPU:1, one launch (start us, length us, event | category | flops | bytes accessed | tf_op | source)
XLA Modules:
  0.0 115.7 jit_solution(16032540050502363850)
XLA Ops:
  1.3 0.8 copy.14
  2.1 0.1 reshape.42
  2.2 0.6 pad_bitcast_fusion.ci
  2.8 1.6 %reshape.44.hid = bf16[160,512]{1,0:T(8,128)(2,1)} reshape(bf16[1,5,8,4,512]{4,3,2,1,0:T(4,128)(2,1)} %param.10) | data formatting | bytes 327680 | tf_op jit(solution)/shard_map/reshape | solution.py:662
  4.4 106.8 %block.1 = (bf16[4,160,128]{2,1,0:T(8,128)(2,1)}, bf16[4,160,128]{2,1,0:T(8,128)(2,1)}, bf16[7,4,2,16,512]{4,3,2,1,0:T(8,128)(2,1)}, f32[16,8,128]{2,1,0:T(8,128)}) custom-call(s32[1]{0:T(128)S(6)} %copy.15.length_ref, s32[8,128]{1,0:T(8,128)} %pad_bitcast_fusion.ci, bf16[160,512]{1,0:T(8,128)(2,1)} %reshape.44.hid, bf16[18,512]{1,0:T(8,128)(2,1)} %emb_ref.1, ...), custom_call_target="tpu_custom_call" | custom-call | tf_op jit(solution)/shard_map/block/pallas_call | solution.py:579
  111.2 2.9 %outputs.1 = (bf16[640,128]{1,0:T(8,128)(2,1)}, bf16[160,512]{1,0:T(8,128)(2,1)}, f32[27,32,512]{2,1,0:T(8,128)}, f32[18,512]{1,0:T(8,128)}, f32[4,128]{1,0:T(4,128)}, /*index=5*/f32[4,128]{1,0:T(4,128)}) custom-call(bf16[4,160,128]{2,1,0:T(8,128)(2,1)} %get-tuple-element.16.dec, bf16[4,160,128]{2,1,0:T(8,128)(2,1)} %get-tuple-element.17.gho, ...), custom_call_target="tpu_custom_call" | custom-call | tf_op jit(solution)/shard_map/outputs/pallas_call | solution.py:649
  114.1 1.6 %reshape.49 = bf16[1,5,8,4,512]{4,3,2,1,0:T(4,128)(2,1)} reshape(bf16[160,512]{1,0:T(8,128)(2,1)} %get-tuple-element.21) | data formatting | bytes 327680 | tf_op jit(solution)/shard_map/reshape | solution.py:667

commit v4 on v3

--- a/solution.py
+++ b/solution.py
@@ -16,6 +16,10 @@
 LP = 512
 G = 7
 MESH = pl.DeviceIdType.MESH
+OFF_R = (0.0, 2.2, 4.6, 9.0, 13.0, 15.5, 18.0)
+OFF_D = (0.0, 0.1, 3.4, 7.4, 11.4, 11.5, 15.0)
+LAG = 1.0
+TAIL = (17.5, 20.6, 21.7, 21.8, 25.3, 26.0, 31.0)
 VM = pl.BlockSpec(memory_space=pltpu.VMEM)
 
 
@@ -101,7 +105,8 @@
             cp.wait_send()
 
 
-N_WIRES = 260
+N_WIRES = 280
+DIRECT = tuple(range(7))
 
 
 def group_sum(x):
@@ -124,9 +129,9 @@
 
 
 def block_body(
-    length_ref, ci, hid, emb_ref, w, gain_ref, bias_ref, cot,
+    length_ref, codes, hid, emb_ref, w, gain_ref, bias_ref, cot,
     dec, gho, fin, smo,
-    epad, fe, up, gcol, cbuf, fsrc, fbuf, u1, u2s, u2, w2s, wts, pat, part, rx1, tx2, rx2, txz, rxz, conv,
+    ci, epad, fe, up, gcol, cbuf, fsrc, fbuf, u1, u2s, u2, w2s, wts, pat, part, rx1, tx2, rx2, txz, rxz, conv,
     ut, nrm, dpr, act, own, dcs, wacc, cw, df, db, drx, dft, d1s, d1, d2s,
     out, qx1, qt2, qx2, sx, rz, sm, xb, zb, ss, rs,
 ):
@@ -156,6 +161,16 @@
 
     length = length_ref[0]
     mk = [jnp.where(t < length, 1.0, 0.0) for t in range(T)]
+    slot = lax.broadcasted_iota(jnp.int32, (WD, 128), 1)
+    column = lax.broadcasted_iota(jnp.int32, (WD, 128), 0)
+    ci[...] = jnp.zeros((8, 128), jnp.int32)
+    for h in range(2):
+        v = jnp.zeros((WD, 128), jnp.int32)
+        for t in range(4 * h, min(T, 4 * h + 4)):
+            for r in range(R):
+                one = jnp.broadcast_to(codes[t, :, r:r + 1], (WD, 128))
+                v = jnp.where(slot // 4 == 8 * (t - 4 * h) + r, one, v)
+        ci[h:h + 1, :] = jnp.sum(jnp.where(slot % 4 == column, v, 0), axis=0, keepdims=True)
     bit = lax.broadcasted_iota(jnp.int32, (128, 128), 0)
     epad[...] = jnp.zeros((128, 512), BF)
     epad[0:CODE_BITS] = emb_ref[...]
@@ -166,7 +181,7 @@
         for t in range(4 * h, min(T, 4 * h + 4)):
             r0 = 32 * (t - 4 * h)
             fe[32 * t:32 * t + 32] = (
-                (nat[r0:r0 + 32] + hid[32 * t:32 * t + 32].astype(F32)) * mk[t]
+                (nat[r0:r0 + 32] + hid[t].astype(F32).reshape(32, 512)) * mk[t]
             ).astype(BF)
     place = placing(0)
     for t in range(T):
@@ -194,13 +209,19 @@
     send("fp", fbuf.at[me], fbuf.at[me], "shard", pair)
     send("w", w.at[:, :, pl.ds(pl.multiple_of(256 * (1 - c), 256), 256)], w2s.at[:, c], "shard", pair)
     w2s[:, c] = w[:, :, pl.ds(pl.multiple_of(256 * c, 256), 256)]
+
+    def relay(dz, dy):
+        frm = sid((z + dz) % 2, (y + 4 - dy) % 4, c)
+        got(("f", dz, dy), fbuf.at[frm])
+        send(("fr", dz, dy), fbuf.at[frm], fbuf.at[frm], "shard", pair)
+
+    relay(0, 1)
+    relay(0, 3)
     got("w", w2s.at[:, 1 - c])
     for dt in range(3):
         wts[dt] = jnp.transpose(w2s[9 * dt:9 * dt + 9].reshape(576, 256).astype(F32)).astype(BF)
-    for dz, dy in steps:
-        frm = sid((z + dz) % 2, (y + 4 - dy) % 4, c)
-        got(("f", dz, dy), fbuf.at[frm])
-        send(("fr", dz, dy), fbuf.at[frm], fbuf.at[frm], "shard", pair)
+    for dz, dy in steps[2:]:
+        relay(dz, dy)
     got("fp", fbuf.at[pair])
     trio = [(0, 1), (1, 0), (1, 1)]
     for dz, dc in trio:
@@ -340,6 +361,10 @@
         dcs[z, y, t] = own[t]
 
     def first_out(kind, get, t0, t1):
+        pack_out(kind, get, t0, t1)
+        send_out(kind, t0, t1)
+
+    def pack_out(kind, get, t0, t1):
         for t in range(t0, t1):
             v = get(t)
             nat = jnp.transpose(jnp.concatenate([v, v, v, v], axis=0))
@@ -350,6 +375,8 @@
                     piece = nat[r0:r0 + 32] * grp[g]
                     acc = piece if acc is None else acc + piece
                 d1s[kind, q, 32 * t:32 * t + 32, :] = acc.astype(BF)
+
+    def send_out(kind, t0, t1):
         for dy in (1, 3, 2):
             yy = (y + dy) % 4
             part_of = pl.ds(32 * t0, 32 * (t1 - t0))
@@ -446,11 +473,20 @@
 
     lo4, hi4 = pl.ds(0, 2), pl.ds(2, 2)
 
+    xfar = xf * 4 + l
+
     def r1(g):
+        if g in DIRECT:
+            send(("r15", g), cw.at[g, xf], qx2.at[2, g], "dp", xfar)
+            send(("r2", g), cw.at[g, xp], qx2.at[0, g], "dp", fwd)
+            send(("r3", g), cw.at[g, xm], qx2.at[1, g], "dp", bwd)
+            return
         send(("r0", g), cw.at[g, xf, lo4], qx1.at[0, g], "dp", fwd)
         send(("r1", g), cw.at[g, xf, hi4], qx1.at[1, g], "dp", bwd)
 
     def r2(g):
+        if g in DIRECT:
+            return
         got(("r0", g), qx1.at[0, g])
         qt2[0, g, 0:2] = (cw[g, xp, 0:2].astype(F32) + qx1[0, g].astype(F32)).astype(BF)
         qt2[0, g, 2:4] = cw[g, xp, 2:4]
@@ -463,7 +499,11 @@
     def r3(g):
         got(("r2", g), qx2.at[0, g])
         got(("r3", g), qx2.at[1, g])
-        sx[g] = (cw[g, x].astype(F32) + qx2[0, g].astype(F32) + qx2[1, g].astype(F32)).astype(BF)
+        tot = cw[g, x].astype(F32) + qx2[0, g].astype(F32) + qx2[1, g].astype(F32)
+        if g in DIRECT:
+            got(("r15", g), qx2.at[2, g])
+            tot = tot + qx2[2, g].astype(F32)
+        sx[g] = tot.astype(BF)
         for k in (3, 2, 1):
             send(("r4", k, g), sx.at[g, (l + k) % 4], rz.at[g, k], "dp", x * 4 + (l + k) % 4)
 
@@ -481,8 +521,12 @@
             got(("r7", k, g), out.at[g, x, (l + 4 - k) % 4])
         send(("r10", g), out.at[g, x], out.at[g, x], "dp", fwd)
         send(("r11", g), out.at[g, x], out.at[g, x], "dp", bwd)
+        if g in DIRECT:
+            send(("r16", g), out.at[g, x], out.at[g, x], "dp", xfar)
 
     def r6(g):
+        if g in DIRECT:
+            return
         got(("r10", g), out.at[g, xm])
         send(("r12", g), out.at[g, xm, lo4], out.at[g, xm, lo4], "dp", fwd)
         got(("r11", g), out.at[g, xp])
@@ -492,8 +536,13 @@
     other = pl.ds(pl.multiple_of(256 * (1 - c), 256), 256)
 
     def r7(g):
-        got(("r12", g), out.at[g, xf, lo4])
-        got(("r13", g), out.at[g, xf, hi4])
+        if g in DIRECT:
+            got(("r10", g), out.at[g, xm])
+            got(("r11", g), out.at[g, xp])
+            got(("r16", g), out.at[g, xf])
+        else:
+            got(("r12", g), out.at[g, xf, lo4])
+            got(("r13", g), out.at[g, xf, hi4])
         send(("r14", g), out.at[g, :, pl.ds(2 * (1 - c), 2)], fin.at[g, :, :, :, mine], "shard", pair)
         fin[g, :, :, :, mine] = out[g, :, pl.ds(2 * c, 2)]
 
@@ -544,7 +593,8 @@
         for d in range(1, NS):
             got(("m3", d), smo.at[(me + NS - d) % NS])
 
-    ev = [(0.1, 0, first_out, (0, lambda t: act[t], 0, T)), (8.2, 0, second_out, (0, dec, 0, T))]
+    ev = [(2.3 + 1.1 * t, 0, pack_out, (0, lambda t: act[t], t, t + 1)) for t in range(T)]
+    ev += [(7.6, 0, send_out, (0, 0, T)), (24.2, 0, second_out, (0, dec, 0, T))]
     for i, t in enumerate(order):
         ev += [
             (2.4 + 1.1 * i, 1, g_near, (t,)), (5.5 + 1.6 * i, 2, g_over, (t,)),
@@ -555,14 +605,15 @@
     ready = (15.22, 15.24, 17.32, 17.34, 19.42, 19.44, 19.46)
     for g in range(G):
         at = ready[g]
-        lag = max(0.0, 15.3 + 1.0 * g - at)
-        for off, n, f in ((0.0, 20, r1), (2.2, 21, r2), (4.6, 22, r3), (9.0, 23, r4), (13.0, 24, r5), (15.5, 25, r6), (18.0, 26, r7)):
+        lag = max(0.0, 15.3 + LAG * g - at)
+        offs = OFF_D if g in DIRECT else OFF_R
+        for off, n, f in zip(offs, range(20, 27), (r1, r2, r3, r4, r5, r6, r7)):
             ev.append((at + off + (lag if off else 0.0), n, f, (g,)))
     get = lambda t: dft[t]
     ev += [
-        (17.5, 30, first_out, (1, get, 2, T)), (20.6, 31, second_out, (1, gho, 2, T)),
-        (21.7, 40, first_out, (1, get, 0, 2)), (21.8, 41, m1, ()),
-        (25.3, 41, second_out, (1, gho, 0, 2)), (26.0, 42, m2, ()), (31.0, 43, m3, ()),
+        (TAIL[0], 30, first_out, (1, get, 2, T)), (TAIL[1], 31, second_out, (1, gho, 2, T)),
+        (TAIL[2], 40, first_out, (1, get, 0, 2)), (TAIL[3], 41, m1, ()),
+        (TAIL[4], 41, second_out, (1, gho, 0, 2)), (TAIL[5], 42, m2, ()), (TAIL[6], 43, m3, ()),
         (37.0, 45, m4, ()), (37.1, 46, third_out, (0, dec, 0, T)),
         (37.2, 47, third_out, (1, gho, 2, T)), (37.3, 48, third_out, (1, gho, 0, 2)),
     ]
@@ -573,7 +624,7 @@
     wires.finish()
 
 
-def block(lengths, ci, hid, emb, w, gain, bias, cot):
+def block(lengths, codes, hid, emb, w, gain, bias, cot):
     v = pltpu.VMEM
     piece = (16, 256)
     return pl.pallas_call(
@@ -586,6 +637,7 @@
         ),
         in_specs=[pl.BlockSpec(memory_space=pltpu.SMEM)] + [VM] * 7, out_specs=(VM,) * 4,
         scratch_shapes=[
+            v((8, 128), jnp.int32),
             v((128, 512), BF), v((160, 512), BF), v((4, 160, 128), BF), v((2, 128, 128), F32),
             v((NS, 8, 128), jnp.int32),
             v((8, 80, 128), BF), v((NS, 80, 128), BF),
@@ -600,12 +652,12 @@
             v((2, T, 32, LP), F32), v((2, T, 32, LP), BF), v((T, 32, LP), BF), v((T, 32, LP), F32),
             v((2, 4, 160, 128), BF), v((2, 4, 160, 128), BF), v((2, 4, 160, 128), BF),
             v((G, 4, 4) + piece, BF), v((2, G, 2) + piece, BF), v((2, G, 4) + piece, BF),
-            v((2, G, 4) + piece, BF), v((G, 4) + piece, BF), v((G, 4) + piece, BF),
+            v((3, G, 4) + piece, BF), v((G, 4) + piece, BF), v((G, 4) + piece, BF),
             v((8, 128), F32), v((4, 8, 128), F32), v((4, 8, 128), F32),
             pltpu.SemaphoreType.DMA((N_WIRES,)), pltpu.SemaphoreType.DMA((N_WIRES,)),
         ],
         compiler_params=params(0), name="block",
-    )(lengths, ci, hid, emb, w, gain, bias, cot)
+    )(lengths, codes, hid, emb, w, gain, bias, cot)
 
 
 def outputs_body(dec, gho, fin, smo, dec_o, gh_o, gc_o, ge_o, gg_o, gb_o):
@@ -630,9 +682,8 @@
     for zz in range(2):
         for h in range(2):
             col = 2 * zz + h
-            gh_o[:, 128 * col:128 * (col + 1)] = gathered(
-                [(gho[2 * zz + g % 2], 2 * h + g // 2) for g in range(4)]
-            ).astype(BF)
+            v = gathered([(gho[2 * zz + g % 2], 2 * h + g // 2) for g in range(4)])
+            gh_o[:, :, :, 128 * col:128 * (col + 1)] = v.reshape(T, R, WD, 128).astype(BF)
     for q in range(4):
         cols = slice(128 * q, 128 * (q + 1))
         for a in range(3):
@@ -649,7 +700,7 @@
     return pl.pallas_call(
         outputs_body,
         out_shape=(
-            s((640, 128), BF), s((160, 512), BF), s((27, 32, 512), F32), s((CODE_BITS, 512), F32),
+            s((640, 128), BF), s((T, R, WD, 512), BF), s((27, 32, 512), F32), s((CODE_BITS, 512), F32),
             s((4, 128), F32), s((4, 128), F32),
         ),
         in_specs=[VM] * 4, out_specs=(VM,) * 6, compiler_params=params(), name="outputs",
@@ -657,14 +708,13 @@
 
 
 def on_device(codes, lengths, hidden, embed, conv_weight, gain, bias, cotangent):
-    ci = jnp.pad(codes.reshape(160), (0, 864)).reshape(8, 128)
     raw = block(
-        lengths, ci, hidden.reshape(160, 512), embed, conv_weight.transpose(1, 0, 2),
+        lengths, codes[0].transpose(0, 2, 1), hidden[0], embed, conv_weight.transpose(1, 0, 2),
         gain.reshape(4, 128), bias.reshape(4, 128), cotangent.reshape(640, 128),
     )
     dec, gh, gc, ge, gg, gb = outputs(*raw)
     return (
-        dec.reshape(1, T, 2 * R, 2 * WD, 128), gh.reshape(1, T, R, WD, 512), gc.transpose(1, 0, 2), ge,
+        dec.reshape(1, T, 2 * R, 2 * WD, 128), gh[None], gc.transpose(1, 0, 2), ge,
         gg.reshape(512), gb.reshape(512),
     )
 

time: 116 us -> 111 us (0.957)
  local copies, waits for them, and re-layouts: 4.75 us -> 0 us
    reshape x4 -> x0, local copies, waits for them, and re-layouts: 3.95 us -> none  [the longest x1 1.63 us: on_device(): gh.reshape(1, T, R, WD, 512)]
where the time goes in v4:
time: 111 us; the launch traced here: 110 us
  Pallas kernels  109 us (98%)
  between operations  1.29 us (1%)
    pallas_call x1, Pallas kernels, block(): pl.pallas_call(block_body, out_shape=(jax.ShapeDtypeStruct((4, 160, 128),...  106 us
    pallas_call x1, Pallas kernels, outputs(): pl.pallas_call(outputs_body, out_shape=(s((640, 128), BF), s((T, R, WD, 5...  2.95 us

profile of v4, /device:TPU:1, one launch (start us, length us, event | category | flops | bytes accessed | tf_op | source)
XLA Modules:
  0.0 110.4 jit_solution(6007251199650653080)
XLA Ops:
  1.3 106.1 %block.1 = (bf16[4,160,128]{2,1,0:T(8,128)(2,1)}, bf16[4,160,128]{2,1,0:T(8,128)(2,1)}, bf16[7,4,2,16,512]{4,3,2,1,0:T(8,128)(2,1)}, f32[16,8,128]{2,1,0:T(8,128)}) custom-call(s32[1]{0:T(128)S(6)} %copy.14.length_ref, s32[5,4,8]{2,1,0:T(4,128)} %bitcast.16, bf16[5,8,4,512]{3,2,1,0:T(4,128)(2,1)} %bitcast.14, bf16[18,512]{1,0:T(8,128)(2,1)} %emb_ref.1, ...), custom_call_target="tpu_custom_call" | custom-call | tf_op jit(solution)/shard_map/block/pallas_call | solution.py:630
  107.4 2.9 %outputs.1 = (bf16[640,128]{1,0:T(8,128)(2,1)}, bf16[5,8,4,512]{3,2,1,0:T(4,128)(2,1)}, f32[27,32,512]{2,1,0:T(8,128)}, f32[18,512]{1,0:T(8,128)}, f32[4,128]{1,0:T(4,128)}, /*index=5*/f32[4,128]{1,0:T(4,128)}) custom-call(bf16[4,160,128]{2,1,0:T(8,128)(2,1)} %get-tuple-element.16.dec, bf16[4,160,128]{2,1,0:T(8,128)(2,1)} %get-tuple-element.17.gho, ...), custom_call_target="tpu_custom_call" | custom-call | tf_op jit(solution)/shard_map/outputs/pallas_call | solution.py:700

commit v5 on v4

--- a/solution.py
+++ b/solution.py
@@ -105,7 +105,9 @@
             cp.wait_send()
 
 
-N_WIRES = 280
+N_WIRES = 290
+SCATTER_DIRECT = (0, 1, 2, 3, 4)
+GATHER_DIRECT = (0, 1, 2, 3, 4)
 DIRECT = tuple(range(7))
 
 
@@ -131,7 +133,7 @@
 def block_body(
     length_ref, codes, hid, emb_ref, w, gain_ref, bias_ref, cot,
     dec, gho, fin, smo,
-    ci, epad, fe, up, gcol, cbuf, fsrc, fbuf, u1, u2s, u2, w2s, wts, pat, part, rx1, tx2, rx2, txz, rxz, conv,
+    ci, epad, fe, up, gcol, cbuf, fsrc, fbuf, u1, u2s, u2, w2s, wts, pat, part, rx1, tx2, rx2, rxf, txz, rxz, conv,
     ut, nrm, dpr, act, own, dcs, wacc, cw, df, db, drx, dft, d1s, d1, d2s,
     out, qx1, qt2, qx2, sx, rz, sm, xb, zb, ss, rs,
 ):
@@ -140,6 +142,7 @@
     x, l = dp // 4, dp % 4
     o = 1 - z
     yp, ym, far = (y + 1) % 4, (y + 3) % 4, (y + 2) % 4
+    far_id = sid(z, far, c)
     up_id, down_id, over, pair = sid(z, yp, c), sid(z, ym, c), sid(o, y, c), sid(z, y, 1 - c)
     xp, xm, xf = (x + 1) % 4, (x + 3) % 4, (x + 2) % 4
     fwd, bwd = xp * 4 + l, xm * 4 + l
@@ -258,10 +261,17 @@
                 acc = d if acc is None else acc + d
         for k in range(8):
             part[k // 4, k % 4, t] = acc[32 * k:32 * (k + 1)].astype(BF)
+        if t in SCATTER_DIRECT:
+            send(("s1a", t), part.at[:, far, t], rxf.at[t], "shard", far_id)
+            send(("s2a", t), part.at[:, yp, t], rx2.at[0, t], "shard", up_id)
+            send(("s2b", t), part.at[:, ym, t], rx2.at[1, t], "shard", down_id)
+            return
         send(("s1a", t), part.at[:, far, t, pl.ds(0, 16)], rx1.at[0, t], "shard", up_id)
         send(("s1b", t), part.at[:, far, t, pl.ds(16, 16)], rx1.at[1, t], "shard", down_id)
 
     def s2(t):
+        if t in SCATTER_DIRECT:
+            return
         got(("s1a", t), rx1.at[0, t])
         tx2[0, t, :, 0:16] = (part[:, yp, t, 0:16].astype(F32) + rx1[0, t].astype(F32)).astype(BF)
         tx2[0, t, :, 16:32] = part[:, yp, t, 16:32]
@@ -274,11 +284,16 @@
     def s3(t):
         got(("s2a", t), rx2.at[0, t])
         got(("s2b", t), rx2.at[1, t])
-        txz[t] = (
-            part[o, y, t].astype(F32) + rx2[0, t, o].astype(F32) + rx2[1, t, o].astype(F32)
-        ).astype(BF)
+        give = part[o, y, t].astype(F32) + rx2[0, t, o].astype(F32) + rx2[1, t, o].astype(F32)
+        if t in SCATTER_DIRECT:
+            got(("s1a", t), rxf.at[t])
+            give = give + rxf[t, o].astype(F32)
+        txz[t] = give.astype(BF)
         send(("s3", t), txz.at[t], rxz.at[t], "shard", over)
-        conv[t] = part[z, y, t].astype(F32) + rx2[0, t, z].astype(F32) + rx2[1, t, z].astype(F32)
+        keep = part[z, y, t].astype(F32) + rx2[0, t, z].astype(F32) + rx2[1, t, z].astype(F32)
+        if t in SCATTER_DIRECT:
+            keep = keep + rxf[t, z].astype(F32)
+        conv[t] = keep
 
     def s4(t):
         got(("s3", t), rxz.at[t])
@@ -319,7 +334,7 @@
             (1.5 * t, 0, comp, (t,)), (2.6 + 2.1 * t, 1, s2, (t,)),
             (5.2 + 2.1 * t, 2, s3, (t,)), (11.0 + 2.1 * t, 3, s4, (t,)),
         ]
-    ev += [(7.0, 9, u_second, ()), (14.5, 9, u_third, ())]
+    ev += [(9.0, 9, u_second, ()), (17.0, 9, u_third, ())]
     run(ev)
 
     count = length.astype(F32) * float(R * WD * NS * 16)
@@ -357,6 +372,8 @@
         send(("g0", t), own.at[t], dcs.at[z, y, t], "shard", over)
         send(("g1", t), own.at[t], dcs.at[z, y, t], "shard", up_id)
         send(("g2", t), own.at[t], dcs.at[z, y, t], "shard", down_id)
+        if t in GATHER_DIRECT:
+            send(("g3", t), own.at[t], dcs.at[z, y, t], "shard", far_id)
     for t in order:
         dcs[z, y, t] = own[t]
 
@@ -410,6 +427,8 @@
             got(("d2", kind, t0, dz, dc), dst.at[2 * ((z + dz) % 2) + (c + dc) % 2, part_of])
 
     def g_near(t):
+        if t in GATHER_DIRECT:
+            return
         got(("g1", t), dcs.at[z, ym, t])
         send(("g3", t), dcs.at[z, ym, t, lo], dcs.at[z, ym, t, lo], "shard", up_id)
         got(("g2", t), dcs.at[z, yp, t])
@@ -419,14 +438,26 @@
         got(("g0", t), dcs.at[o, y, t])
         send(("g5", t), dcs.at[o, y, t], dcs.at[o, y, t], "shard", up_id)
         send(("g6", t), dcs.at[o, y, t], dcs.at[o, y, t], "shard", down_id)
+        if t in GATHER_DIRECT:
+            send(("g7", t), dcs.at[o, y, t], dcs.at[o, y, t], "shard", far_id)
 
     def g_far(t):
+        if t in GATHER_DIRECT:
+            return
         got(("g5", t), dcs.at[o, ym, t])
         send(("g7", t), dcs.at[o, ym, t, lo], dcs.at[o, ym, t, lo], "shard", up_id)
         got(("g6", t), dcs.at[o, yp, t])
         send(("g8", t), dcs.at[o, yp, t, hi], dcs.at[o, yp, t, hi], "shard", down_id)
 
     def g_done(t):
+        if t in GATHER_DIRECT:
+            got(("g1", t), dcs.at[z, ym, t])
+            got(("g2", t), dcs.at[z, yp, t])
+            got(("g3", t), dcs.at[z, far, t])
+            got(("g5", t), dcs.at[o, ym, t])
+            got(("g6", t), dcs.at[o, yp, t])
+            got(("g7", t), dcs.at[o, far, t])
+            return
         got(("g3", t), dcs.at[z, far, t, lo])
         got(("g4", t), dcs.at[z, far, t, hi])
         got(("g7", t), dcs.at[o, far, t, lo])
@@ -593,11 +624,11 @@
         for d in range(1, NS):
             got(("m3", d), smo.at[(me + NS - d) % NS])
 
-    ev = [(2.3 + 1.1 * t, 0, pack_out, (0, lambda t: act[t], t, t + 1)) for t in range(T)]
-    ev += [(7.6, 0, send_out, (0, 0, T)), (24.2, 0, second_out, (0, dec, 0, T))]
+    ev = [(2.0 + 0.5 * t, 0, pack_out, (0, lambda t: act[t], t, t + 1)) for t in range(T)]
+    ev += [(9.6, 0, send_out, (0, 0, T)), (24.2, 0, second_out, (0, dec, 0, T))]
     for i, t in enumerate(order):
         ev += [
-            (2.4 + 1.1 * i, 1, g_near, (t,)), (5.5 + 1.6 * i, 2, g_over, (t,)),
+            (2.4 + 1.1 * i, 1, g_near, (t,)), (4.5 + 1.2 * i, 2, g_over, (t,)),
             (8.5 + 1.6 * i, 3, g_far, (t,)), (11.0 + 2.1 * i, 4, g_done, (t,)),
             (11.0 + 2.1 * i, 5, wgrad, (t,)), (11.1 + 2.1 * i, 30, dgrad, (t,)),
             (13.2 + 2.1 * i, 7, dsum, (t,)),
@@ -645,6 +676,7 @@
             v((27, 2, 32, 256), BF), v((3, 256, 576), BF),
             v((T, 576, LP), BF), v((2, 4, T, 32, LP), BF),
             v((2, T, 2, 16, LP), BF), v((2, T, 2, 32, LP), BF), v((2, T, 2, 32, LP), BF),
+            v((T, 2, 32, LP), BF),
             v((T, 32, LP), BF), v((T, 32, LP), BF), v((T, 32, LP), F32),
             v((T, 32, LP), F32), v((T, 32, LP), F32), v((T, 32, LP), F32), v((T, 32, LP), F32),
             v((T, 32, LP), BF), v((2, 4, T, 32, LP), BF), v((3, 576, 256), F32),

time: 111 us -> 107 us (0.964)
  Pallas kernels: 109 us -> 106 us
    pallas_call x1, Pallas kernels: 106 us -> 103 us  [block(): pl.pallas_call(block_body, out_shape=(jax.ShapeDtypeStruct((4, 160, 128),...]
where the time goes in v5:
time: 107 us
  Pallas kernels  106 us (99%)
  between operations  1.29 us (1%)
    pallas_call x1, Pallas kernels, block(): pl.pallas_call(block_body, out_shape=(jax.ShapeDtypeStruct((4, 160, 128),...  103 us
    pallas_call x1, Pallas kernels, outputs(): pl.pallas_call(outputs_body, out_shape=(s((640, 128), BF), s((T, R, WD, 5...  2.95 us

profile of v5, /device:TPU:1, one launch (start us, length us, event | category | flops | bytes accessed | tf_op | source)
XLA Modules:
  0.0 106.8 jit_solution(2083055619863349219)
XLA Ops:
  1.3 102.6 %block.1 = (bf16[4,160,128]{2,1,0:T(8,128)(2,1)}, bf16[4,160,128]{2,1,0:T(8,128)(2,1)}, bf16[7,4,2,16,512]{4,3,2,1,0:T(8,128)(2,1)}, f32[16,8,128]{2,1,0:T(8,128)}) custom-call(s32[1]{0:T(128)S(6)} %copy.14.length_ref, s32[5,4,8]{2,1,0:T(4,128)} %bitcast.16, bf16[5,8,4,512]{3,2,1,0:T(4,128)(2,1)} %bitcast.14, bf16[18,512]{1,0:T(8,128)(2,1)} %emb_ref.1, ...), custom_call_target="tpu_custom_call" | custom-call | tf_op jit(solution)/shard_map/block/pallas_call | solution.py:661
  103.9 2.9 %outputs.1 = (bf16[640,128]{1,0:T(8,128)(2,1)}, bf16[5,8,4,512]{3,2,1,0:T(4,128)(2,1)}, f32[27,32,512]{2,1,0:T(8,128)}, f32[18,512]{1,0:T(8,128)}, f32[4,128]{1,0:T(4,128)}, /*index=5*/f32[4,128]{1,0:T(4,128)}) custom-call(bf16[4,160,128]{2,1,0:T(8,128)(2,1)} %get-tuple-element.16.dec, bf16[4,160,128]{2,1,0:T(8,128)(2,1)} %get-tuple-element.17.gho, ...), custom_call_target="tpu_custom_call" | custom-call | tf_op jit(solution)/shard_map/outputs/pallas_call | solution.py:732
